TPU v7x, 128 devices: a whole 4x4x4 slice. The times are simulated.
128 devices in a mesh: dp: 4 (over z), cls: 32 (over y, x, core).
Axes of the slice: x: 4, y: 4, z: 4, core: 2. Of those that a mesh axis runs over, the one named last changes fastest.
Arguments:
- embeddings: bfloat16 [8192, 512], P(('dp', 'cls')), may hold values from -6 to 6
- labels: int32 [8192], P('dp'), may hold values from 0 to 65535
- centres: bfloat16 [131072, 512], P('cls'), may hold values from -0.25 to 0.25
- momentum: float32 [131072, 512], P('cls'), may hold values from -3 to 3
- sample_home: int32 [65536, 1], P('cls'), may hold values from 0 to 31; in each aligned block of 2048 rows (0 to 2047, 2048 to 4095, ...) at most 128 rows name the same one
- sample_row: int32 [65536], P('cls'), may hold values from 0 to 4095
Outputs:
- emb_grad: float32 [8192, 512], P(('dp', 'cls'))
- momentum_new: float32 [131072, 512], P('cls')
- centres_new: bfloat16 [131072, 512], P('cls')
Inputs may be any that keep to these rules, and one draw needn't show every extreme that they name: Among the 2048 sampled columns of one class tile (aligned blocks of sample_home), at most 128 name the same home shard, and in every draw some home shard supplies exactly 128 columns of some tile.
All inputs are finite; a program needn't handle non-finite values.
Results may differ from a plain program's by a relative error of at most 0.014.
Values may be sent and summed in bfloat16 or wider, within the bound.
A program may use at most 128 MiB of HBM per device.

v0:
```python
import jax
import jax.numpy as jnp
from jax import lax
from jax.sharding import Mesh
from jax.sharding import PartitionSpec as P

CLS = ("cls_0", "cls_1", "cls_2")
DP_CLS = ("dp", "cls_0", "cls_1", "cls_2")


eps = 1e-06
logit_scale = 64.0
margin = 0.35
momentum_rate = 0.9
learn_rate = 0.1
weight_decay = 0.0005


def laid_out(parts, dim):
    parts = jnp.moveaxis(parts, 0, dim)
    shape = parts.shape
    return parts.reshape(*shape[:dim], shape[dim] * shape[dim + 1], *shape[dim + 2 :])


def sent_to_all(value, axis):
    copies = jnp.broadcast_to(value, (lax.axis_size(axis), *value.shape))
    return lax.all_to_all(copies, axis, split_axis=0, concat_axis=0, tiled=True)


def gather_directly(value, axis, dim):
    return laid_out(sent_to_all(value, axis), dim)


def of_everyone(value, axis):
    everything = sent_to_all(value, axis)
    return jnp.sum(everything, axis=0)


def split_up(value, dim, length):
    before, after = (value.shape[:dim], value.shape[dim + 1 :])
    return jnp.moveaxis(value.reshape(*before, length, -1, *after), dim, 0)


def sent_and_summed(value, axis, dim):
    parts = split_up(value, dim, lax.axis_size(axis))
    arrived = lax.all_to_all(parts, axis, split_axis=0, concat_axis=0, tiled=True)
    return arrived.astype(jnp.float32).sum(axis=0)


def exchange_in_order(parts, axes, turns):
    shape = [lax.axis_size(a) for a in axes]
    parts = parts.reshape(*shape, *parts.shape[1:])
    for k in turns:
        parts = lax.all_to_all(parts, axes[k], split_axis=k, concat_axis=k, tiled=True)
    return parts.reshape(-1, *parts.shape[len(axes) :])


def two_step_exchange(value, groups, turns, split_dim, concat_dim):
    length = lax.axis_size(groups[0]) * lax.axis_size(groups[1])
    parts = split_up(value, split_dim, length)
    return laid_out(exchange_in_order(parts, groups, turns), concat_dim)


def body(embeddings, labels, centres, momentum, sample_home, sample_row):
    shards = lax.axis_size(CLS)
    sampled_here = sample_row.shape[0]
    capacity = 2 * sampled_here // shards
    width = embeddings.shape[1]
    home_rows = centres.shape[0]
    xfloat = embeddings.astype(jnp.float32)
    row_norm = jnp.sqrt(jnp.sum(xfloat * xfloat, axis=1, keepdims=True) + eps)
    unit_centres = xfloat / row_norm
    normalized_embedding = unit_centres.astype(jnp.bfloat16)
    collected_centres = gather_directly(normalized_embedding, CLS, 0)
    home_shard = sample_home[:, 0]
    shard_ids = jnp.arange(shards, dtype=jnp.int32)
    home_onehot = (home_shard[:, None] == shard_ids[None, :]).astype(jnp.int32)
    slot_rank = jnp.sum(jnp.cumsum(home_onehot, axis=0) * home_onehot, axis=1) - 1
    request = jnp.zeros((shards, capacity), jnp.int32).at[home_shard, slot_rank].set(sample_row)
    incoming = lax.all_to_all(request, CLS, split_axis=0, concat_axis=0, tiled=True)
    replies = centres[incoming]
    arrived = lax.all_to_all(replies, CLS, split_axis=0, concat_axis=0, tiled=True)
    fetched = arrived[home_shard, slot_rank]
    wfloat = fetched.astype(jnp.float32)
    col_norm = jnp.sqrt(jnp.sum(wfloat * wfloat, axis=1, keepdims=True) + eps)
    wunit = wfloat / col_norm
    what = wunit.astype(jnp.bfloat16)
    cosine = lax.dot_general(
        collected_centres, what, (((1,), (1,)), ((), ())), preferred_element_type=jnp.float32
    )
    tile_index = lax.axis_index(CLS)
    local_label = labels - tile_index * sampled_here
    column_ids = jnp.arange(sampled_here, dtype=jnp.int32)
    target = (local_label[:, None] == column_ids[None, :]).astype(jnp.float32)
    exp_logit = jnp.exp(logit_scale * (cosine - margin * target))
    denominator = of_everyone(jnp.sum(exp_logit, axis=1), CLS)
    grad_logit = (logit_scale * (exp_logit / denominator[:, None] - target)).astype(jnp.bfloat16)
    dunit = sent_and_summed(
        jnp.dot(grad_logit, what, preferred_element_type=jnp.float32).astype(jnp.bfloat16), CLS, 0
    )
    emb_grad = (
        dunit - unit_centres * jnp.sum(unit_centres * dunit, axis=1, keepdims=True)
    ) / row_norm
    dwhat = lax.dot_general(
        grad_logit, collected_centres, (((0,), (0,)), ((), ())), preferred_element_type=jnp.float32
    )
    dfetched = (dwhat - wunit * jnp.sum(wunit * dwhat, axis=1, keepdims=True)) / col_norm
    packed_buffer = (
        jnp.zeros((shards, capacity, width), jnp.float32).at[home_shard, slot_rank].set(dfetched)
    )
    share_part = sent_and_summed(packed_buffer.astype(jnp.bfloat16), "dp", 1)
    received = two_step_exchange(
        share_part.astype(jnp.bfloat16), (("cls_0", "cls_1"), "cls_2"), (1, 0), 0, 0
    ).astype(share_part.dtype)
    returned = lax.all_gather(received.astype(jnp.bfloat16), "dp", axis=1, tiled=True).astype(
        received.dtype
    )
    centre_grad = (
        jnp.zeros((home_rows, width), jnp.float32)
        .at[incoming.reshape(-1)]
        .add(returned.reshape(-1, width))
    )
    centre_float = centres.astype(jnp.float32)
    momentum_new = momentum_rate * momentum + centre_grad + weight_decay * centre_float
    centres_new = (centre_float - learn_rate * momentum_new).astype(jnp.bfloat16)
    return (emb_grad, momentum_new, centres_new)


def solution(mesh):
    torus = Mesh(mesh.devices.reshape(mesh.shape["dp"], 4, 4, 2), ("dp", "cls_0", "cls_1", "cls_2"))
    return jax.shard_map(
        body,
        mesh=torus,
        in_specs=(P(DP_CLS, None), P("dp"), P(CLS, None), P(CLS, None), P(CLS, None), P(CLS)),
        out_specs=(P(DP_CLS, None), P(CLS, None), P(CLS, None)),
        check_vma=False,
    )
```

profile of v0, /device:TPU:0, one launch (start us, length us, event | category | flops | bytes accessed | tf_op | source)
XLA Modules:
  0.0 419.1 jit_solution(11791057206995185234)
XLA Ops:
  7.2 0.7 fusion.11
  7.9 9.1 %reduce-window.6 = s32[32,16,128]{2,1,0:T(8,128)S(1)} reduce-window(s32[32,16,128]{2,1,0:T(8,128)S(1)} %fusion.11, s32[]{:T(128)} %constant.20.clone.1), window={size=1x1x128 pad=0_0x0_0x127_0}, to_apply=%region_1.0 | reduce-window | flops 8323072 | bytes 524292 | tf_op jit(solution)/shard_map/reduce-window
  17.0 0.1 slice.12
  17.1 0.2 copy.42
  17.3 0.2 reduce-window.9
  17.5 0.1 broadcast_add_fusion
  17.7 0.8 fusion.10
  18.5 0.7 shift-left_or_fusion
  19.2 0.8 and_reduce_fusion
  20.0 0.7 multiply_reduce_fusion.2
  20.8 8.2 %scatter_custom_fusion.1 = s32[4096]{0:T(1024)S(1)} fusion(s32[2048]{0:T(1024)S(1)} %broadcast_select_fusion, s32[2048]{0:T(1024)} %param.11, s32[]{:T(128)} %constant.20.clone.1), kind=kCustom, calls=%fused_computation.48 | custom fusion | bytes 16896
  29.0 14.6 %all_to_all.48 = s32[32,1,128]{2,1,0:T(1,128)S(1)} all-to-all(s32[32,1,128]{2,1,0:T(1,128)S(1)} %bitcast.59), channel_id=1, replica_groups=mesh['dp'=4,'cls_0'=4,'cls_1'=4,'cls_2'=2] {'cls_0','cls_1','cls_2'}, dimensions={0} | all-to-all | bytes 32768 | tf_op jit(solution)/shard_map/all_to_all | solution.py:80
  43.6 20.2 %gather_fusion = bf16[4096,512]{1,0:T(8,128)(2,1)} fusion(bf16[4096,512]{1,0:T(8,128)(2,1)} %param.8, s32[4096]{0:T(1024)S(1)} %fusion.14), kind=kCustom, calls=%fused_computation | custom fusion | bytes 8404992 | tf_op jit(solution)/shard_map/gather | solution.py:81
  63.7 5.0 %all-to-all-start.2 = ((bf16[32,128,512]{2,1,0:T(8,128)(2,1)}), bf16[32,128,512]{2,1,0:T(8,128)(2,1)}, u32[]{:S(2)}, u32[]{:S(2)}) async-start(bf16[32,128,512]{2,1,0:T(8,128)(2,1)} %bitcast.46), calls=%async_computation.2 | async-start | bytes 8388608 | tf_op jit(solution)/shard_map/all_to_all | solution.py:82
  68.7 0.1 fusion.12
  68.9 0.1 fusion.17
  69.0 53.2 %all-to-all-done.2 = bf16[32,128,512]{2,1,0:T(8,128)(2,1)} async-done(((bf16[32,128,512]{2,1,0:T(8,128)(2,1)}), bf16[32,128,512]{2,1,0:T(8,128)(2,1)}, u32[]{:S(2)}, u32[]{:S(2)}) %all-to-all-start.2) | async-done | bytes 4194336 | tf_op jit(solution)/shard_map/all_to_all | solution.py:82
  122.2 1.6 broadcast_in_dim.6
  123.8 4.8 %all-to-all-start = ((bf16[32,64,512]{2,1,0:T(8,128)(2,1)}), bf16[32,64,512]{2,1,0:T(8,128)(2,1)}, u32[]{:S(2)}, u32[]{:S(2)}) async-start(bf16[32,64,512]{2,1,0:T(8,128)(2,1)} %broadcast_in_dim.6), calls=%async_computation | async-start | bytes 4194304 | tf_op jit(solution)/shard_map/all_to_all | solution.py:27
  128.6 37.0 %gather_fusion.1 = bf16[2048,512]{1,0:T(8,128)(2,1)} fusion(bf16[32,128,512]{2,1,0:T(8,128)(2,1)} %all-to-all-done.2, s32[2048]{0:T(1024)S(1)} %bitcast.45), kind=kCustom, calls=%fused_computation.1 | custom fusion | bytes 4210688 | tf_op jit(solution)/shard_map/gather | solution.py:83
  165.6 2.9 copy.36
  168.5 0.5 fusion.5
  169.0 12.3 %fusion = (f32[2048]{0:T(1024)S(1)}, f32[2048,2048]{0,1:T(8,128)}) fusion(s32[2048]{0:T(1024)S(1)} %broadcast_subtract_fusion, bf16[2048,512]{1,0:T(8,128)(2,1)} %bitcast, f32[2048]{0:T(1024)S(1)} %add_sqrt_fusion, bf16[2048,512]{0,1:T(8,128)(2,1)S(1)} %copy.36), kind=kOutput, calls=%fused_computation.8 | convolution fusion | flops 4319082496 | bytes 20996096 | tf_op jit(solution)/shard_map/dot_general | solution.py:88
  181.2 0.1 broadcast_in_dim.7
  181.4 15.9 %all_to_all.49 = f32[32,1,2048]{2,1,0:T(1,128)S(1)} all-to-all(f32[32,1,2048]{2,1,0:T(1,128)S(1)} %broadcast_in_dim.7), channel_id=1, replica_groups=mesh['dp'=4,'cls_0'=4,'cls_1'=4,'cls_2'=2] {'cls_0','cls_1','cls_2'}, dimensions={0} | all-to-all | bytes 524288 | tf_op jit(solution)/shard_map/all_to_all | solution.py:27
  197.3 0.2 reduce_sum.88
  197.4 9.3 %multiply_convert_fusion = bf16[2048,2048]{0,1:T(8,128)(2,1)S(1)} fusion(f32[2048,2048]{0,1:T(8,128)} %get-tuple-element.9, f32[2048]{0:T(1024)S(1)} %reduce_sum.88, s32[2048]{0:T(1024)S(1)} %broadcast_subtract_fusion), kind=kLoop, calls=%fused_computation.5 | loop fusion | flops 37748736 | bytes 25182208 | tf_op jit(solution)/shard_map/convert_element_type | solution.py:97
  206.7 8.3 %multiply_reduce_fusion = (f32[2048]{0:T(1024)S(1)}, f32[2048,512]{0,1:T(8,128)S(1)}) fusion(f32[2048]{0:T(1024)S(1)} %add_sqrt_fusion, bf16[2048,512]{0,1:T(8,128)(2,1)S(1)} %copy.36, bf16[2048,2048]{0,1:T(8,128)(2,1)S(1)} %multiply_convert_fusion, bf16[2048,512]{1,0:T(8,128)(2,1)} %bitcast), kind=kOutput, calls=%fused_computation.22 | convolution fusion | flops 4299159552 | bytes 16793600 | tf_op jit(solution)/shard_map/dot_general | solution.py:104
  215.1 2.9 subtract_divide_fusion
  218.0 5.3 %copy.38 = f32[2048,512]{1,0:T(8,128)} copy(f32[2048,512]{0,1:T(8,128)} %subtract_divide_fusion) | data formatting | bytes 8388608 | tf_op jit(solution)/shard_map/div | solution.py:107
  223.3 13.4 %scatter_custom_fusion.2 = f32[4096,512]{1,0:T(8,128)} fusion(s32[2048]{0:T(1024)S(1)} %broadcast_select_fusion, f32[2048,512]{1,0:T(8,128)} %copy.38, f32[]{:T(128)} %constant.18.clone.1), kind=kCustom, calls=%fused_computation.19 | custom fusion | bytes 8389120
  236.7 3.9 convert_element_type.55
  240.6 0.3 copy.47
  240.9 54.5 %all_to_all.50 = bf16[4,32,32,512]{3,2,1,0:T(8,128)(2,1)} all-to-all(bf16[4,32,32,512]{3,2,1,0:T(8,128)(2,1)S(1)} %bitcast.48), channel_id=1, replica_groups=mesh['dp'=4,'cls_0'=4,'cls_1'=4,'cls_2'=2] {'dp'}, dimensions={0} | all-to-all | bytes 8388608 | tf_op jit(solution)/shard_map/all_to_all | solution.py:46
  295.4 3.1 reduce_sum.92
  298.5 0.1 copy.40
  298.6 4.6 %all_to_all.51 = bf16[16,2,1,32,512]{4,3,0,2,1:T(8,128)(2,1)S(1)} all-to-all(bf16[16,2,1,32,512]{4,3,0,2,1:T(8,128)(2,1)S(1)} %copy.40), channel_id=1, replica_groups=mesh['dp'=4,'cls_0'=4,'cls_1'=4,'cls_2'=2] {'cls_2'}, dimensions={1} | all-to-all | bytes 2097152 | tf_op jit(solution)/shard_map/all_to_all | solution.py:54
  303.2 0.1 copy.41
  303.3 21.1 %all_to_all.52 = bf16[16,2,1,32,512]{4,3,1,2,0:T(8,128)(2,1)} all-to-all(bf16[16,2,1,32,512]{4,3,1,2,0:T(8,128)(2,1)S(1)} %copy.41), channel_id=1, replica_groups=mesh['dp'=4,'cls_0'=4,'cls_1'=4,'cls_2'=2] {'cls_0','cls_1'}, dimensions={0} | all-to-all | bytes 2097152 | tf_op jit(solution)/shard_map/all_to_all | solution.py:54
  324.4 9.4 %convolution_convert_fusion = bf16[2048,512]{1,0:T(8,128)(2,1)} fusion(bf16[2048,2048]{0,1:T(8,128)(2,1)} %copy-done, f32[2048]{0:T(1024)S(1)} %add_sqrt_fusion, bf16[2048,512]{0,1:T(8,128)(2,1)S(1)} %copy.36), kind=kOutput, calls=%fused_computation.24 | convolution fusion | flops 4299161600 | bytes 12591104 | tf_op jit(solution)/shard_map/dot_general | solution.py:99
  333.8 4.0 all-to-all-start.4
  337.8 9.6 %fusion.1 = f32[4096,512]{1,0:T(8,128)} fusion(bf16[4096,512]{1,0:T(8,128)(2,1)} %param.8, f32[4096,512]{1,0:T(8,128)} %param.9), kind=kLoop, calls=%fused_computation.11 | loop fusion | flops 8388608 | bytes 20971520 | tf_op jit(solution)/shard_map/add.2
  347.5 20.3 %all-to-all-done.4 = bf16[32,64,512]{2,1,0:T(8,128)(2,1)S(1)} async-done(((bf16[32,64,512]{2,1,0:T(8,128)(2,1)}), bf16[32,64,512]{2,1,0:T(8,128)(2,1)S(1)}, u32[]{:S(2)}, u32[]{:S(2)}) %all-to-all-start.4) | async-done | bytes 2097184 | tf_op jit(solution)/shard_map/all_to_all | solution.py:46
  367.8 0.3 convert_reduce_fusion
  368.1 0.2 multiply_reduce_fusion.1
  368.3 0.8 subtract_divide_fusion.1
  369.1 35.0 %scatter_custom_fusion = f32[4096,512]{1,0:T(8,128)} fusion(f32[4096,512]{1,0:T(8,128)} %fusion.1, s32[4096]{0:T(1024)S(1)} %bitcast.62, bf16[4096,512]{1,0:T(8,128)(2,1)} %bitcast.49), kind=kCustom, calls=%fused_computation.13 | custom fusion | flops 4194304 | bytes 12582912 | tf_op jit(solution)/shard_map/scatter-add | solution.py:121
  404.1 8.1 %fusion.2 = bf16[4096,512]{1,0:T(8,128)(2,1)} fusion(bf16[4096,512]{1,0:T(8,128)(2,1)} %param.8, f32[4096,512]{1,0:T(8,128)} %scatter_custom_fusion), kind=kLoop, calls=%fused_computation.12 | loop fusion | flops 8388608 | bytes 16777216 | tf_op jit(solution)/shard_map/convert_element_type | solution.py:125
  (17 shorter events, 0.1 us)
Async XLA Ops:
  63.7 5.0 %copy-start.1 = (bf16[64,512]{1,0:T(8,128)(2,1)S(1)}, bf16[64,512]{1,0:T(8,128)(2,1)}, u32[]{:S(2)}) copy-start(bf16[64,512]{1,0:T(8,128)(2,1)} %param.6) | copy-start | bytes 196612
  63.7 58.5 %all-to-all-start.2 = ((bf16[32,128,512]{2,1,0:T(8,128)(2,1)}), bf16[32,128,512]{2,1,0:T(8,128)(2,1)}, u32[]{:S(2)}, u32[]{:S(2)}) async-start(bf16[32,128,512]{2,1,0:T(8,128)(2,1)} %bitcast.46), calls=%async_computation.2 | async-start | bytes 8388608 | tf_op jit(solution)/shard_map/all_to_all | solution.py:82
  68.7 59.9 %copy-start.2 = (s32[2048]{0:T(1024)S(1)}, s32[2048]{0:T(1024)}, u32[]{:S(2)}) copy-start(s32[2048]{0:T(1024)} %param.7) | copy-start | bytes 24580
  123.8 45.2 %all-to-all-start = ((bf16[32,64,512]{2,1,0:T(8,128)(2,1)}), bf16[32,64,512]{2,1,0:T(8,128)(2,1)}, u32[]{:S(2)}, u32[]{:S(2)}) async-start(bf16[32,64,512]{2,1,0:T(8,128)(2,1)} %broadcast_in_dim.6), calls=%async_computation | async-start | bytes 4194304 | tf_op jit(solution)/shard_map/all_to_all | solution.py:27
  128.5 240.5 %all-gather.2.cloned.1.call-start = ((), (), s32[]{:S(2)}) async-start(), calls=%async_computation.8 | async-start | bytes 5242880 | tf_op jit(solution)/shard_map/all_gather | solution.py:115
  206.7 8.3 %copy-start = (bf16[2048,2048]{0,1:T(8,128)(2,1)}, bf16[2048,2048]{0,1:T(8,128)(2,1)S(1)}, u32[]{:S(2)}) copy-start(bf16[2048,2048]{0,1:T(8,128)(2,1)S(1)} %multiply_convert_fusion) | copy-start | bytes 25165828
  333.8 34.0 %all-to-all-start.4 = ((bf16[32,64,512]{2,1,0:T(8,128)(2,1)}), bf16[32,64,512]{2,1,0:T(8,128)(2,1)S(1)}, u32[]{:S(2)}, u32[]{:S(2)}) async-start(bf16[32,64,512]{2,1,0:T(8,128)(2,1)} %bitcast.52), calls=%async_computation.4 | async-start | bytes 4194304 | tf_op jit(solution)/shard_map/all_to_all | solution.py:46
Sparse Core Ops, SparseCore 0:
  324.5 44.0 all-gather.1
where the time goes:
time: 421 us; the launch traced here: 419 us
  blocking collectives  111 us (26%)
  local copies, waits for them, and re-layouts  89.6 us (21%)
  other arithmetic  87.3 us (21%)
  waiting for transfers between devices  73.6 us (17%)
  matrix products  30 us (7%)
  between operations  14.2 us (3%)
  starting transfers between devices  13.8 us (3%)
    all_to_all x1, blocking collectives, sent_and_summed(): lax.all_to_all(parts, axis, split_axis=0, concat_axis=0, tiled=True)  54.5 us
    all_to_all x1, waiting for transfers between devices, body(): lax.all_to_all(replies, CLS, split_axis=0, concat_axis=0, tiled=True)  53.2 us
    gather x2, local copies, waits for them, and re-layouts, body(): fetched = arrived[home_shard, slot_rank]  39.9 us
    scatter-add x1, other arithmetic, body(): centre_grad = jnp.zeros((home_rows, width), jnp.float32).at[incoming.resh...  35 us
    all_to_all x2, blocking collectives, exchange_in_order(): lax.all_to_all(parts, axes[k], split_axis=k, concat_axis=k, tiled=True)  25.7 us
    unnamed x8, local copies, waits for them, and re-layouts  21.6 us
    all_to_all x1, waiting for transfers between devices, sent_and_summed(): lax.all_to_all(parts, axis, split_axis=0, concat_axis=0, tiled=True)  20.3 us
    gather x1, local copies, waits for them, and re-layouts, body(): replies = centres[incoming]  20.2 us
  transfers between devices with their start and end apart: 4, of which 2 were waited for; matrix products, arithmetic and copies ran while one was open for 15% of the time, Pallas kernels for 0%

commit v1 on v0

v1 whole, which is shorter than its diff:
```python
import functools

import jax
import jax.numpy as jnp
from jax import lax
from jax.experimental import pallas as pl
from jax.experimental.pallas import tpu as pltpu
from jax.sharding import Mesh
from jax.sharding import PartitionSpec as P

CLS = ("cls_0", "cls_1", "cls_2")
DP_CLS = ("dp", "cls_0", "cls_1", "cls_2")

eps = 1e-06
logit_scale = 64.0
margin = 0.35
momentum_rate = 0.9
learn_rate = 0.1
weight_decay = 0.0005
BF16 = jnp.bfloat16
F32 = jnp.float32


def matmul(a, b):
    return jnp.dot(a, b, preferred_element_type=F32)


def plan_columns(home, row, groups, group, shards, slots):
    columns = home.shape[0]
    block = 128
    blocks = columns // block
    onehot = (home[:, None] == jnp.arange(shards)[None, :]).astype(BF16)
    cut = onehot.reshape(blocks, block, shards)
    lower = jnp.tril(jnp.ones((block, block), BF16), -1)
    within = jnp.einsum("ij,bjh->bih", lower, cut, preferred_element_type=F32)
    totals = jnp.sum(cut.astype(F32), axis=1)
    before = matmul(jnp.tril(jnp.ones((blocks, blocks), BF16), -1), totals.astype(BF16))
    count = jnp.sum(totals, axis=0)
    offset = jnp.sum(
        jnp.where(jnp.arange(shards)[:, None] < jnp.arange(shards)[None, :], count[:, None], 0.0), axis=0
    )
    table = (within + before[:, None, :] + offset[None, None, :]).reshape(columns, shards)
    onehot32 = onehot.astype(F32)
    place = jnp.sum(table * onehot32, axis=1).astype(jnp.int32)
    first = ((offset.astype(jnp.int32) - group + groups - 1) // groups).astype(F32)
    start = jnp.sum(first[None, :] * onehot32, axis=1).astype(jnp.int32)
    mine = place % groups == group
    kept = jnp.where(mine, place // groups, -1)
    slot = jnp.where(mine, home * slots + place // groups - start, -1)

    def digits(*values):
        parts = [part for value in values for part in (value // 64, value % 64)]
        return jnp.stack(parts, axis=1).astype(BF16)

    def whole(parts, i):
        return (parts[:, 2 * i] * 64 + parts[:, 2 * i + 1]).astype(jnp.int32)

    by_slot = (jnp.arange(shards * slots)[:, None] == slot[None, :]).astype(BF16)
    request = whole(matmul(by_slot, digits(row)), 0)
    by_kept = (jnp.arange(columns // groups)[:, None] == kept[None, :]).astype(BF16)
    found = matmul(by_kept, digits(slot, jnp.arange(columns)))
    return request, whole(found, 0), whole(found, 1)


def update_kernel(index_ref, returned_ref, momentum_ref, centres_ref, momentum_out, centres_out):
    rows = momentum_ref.shape[0]
    slots = returned_ref.shape[0]
    first = pl.program_id(0) * rows
    ids = lax.broadcasted_iota(jnp.int32, (rows, slots), 0) + first
    pick = jnp.where(ids == index_ref[...], 1.0, 0.0).astype(BF16)
    grad = jnp.dot(pick, returned_ref[...], preferred_element_type=F32)
    centre = centres_ref[...].astype(F32)
    momentum = momentum_rate * momentum_ref[...] + grad + weight_decay * centre
    momentum_out[...] = momentum
    centres_out[...] = (centre - learn_rate * momentum).astype(BF16)


def update(index, returned, momentum, centres, rows=512):
    slots, width = returned.shape
    homes = centres.shape[0]
    part = pl.BlockSpec((rows, width), lambda i: (i, 0))
    return pl.pallas_call(
        update_kernel,
        grid=(homes // rows,),
        in_specs=[
            pl.BlockSpec((1, slots), lambda i: (0, 0)),
            pl.BlockSpec((slots, width), lambda i: (0, 0)),
            part,
            part,
        ],
        out_specs=[part, part],
        out_shape=[
            jax.ShapeDtypeStruct((homes, width), F32),
            jax.ShapeDtypeStruct((homes, width), BF16),
        ],
        compiler_params=pltpu.CompilerParams(vmem_limit_bytes=48 * 2**20),
        cost_estimate=pl.CostEstimate(
            flops=2 * homes * slots * width, bytes_accessed=16 * homes * width, transcendentals=0
        ),
        name="update",
    )(index.reshape(1, slots), returned, momentum, centres)


def body(embeddings, labels, centres, momentum, sample_home, sample_row):
    shards = lax.axis_size(CLS)
    groups = lax.axis_size("dp")
    group = lax.axis_index("dp")
    tile = lax.axis_index(CLS)
    columns = sample_row.shape[0]
    slots = 2 * columns // shards // groups
    width = embeddings.shape[1]
    homes = centres.shape[0]

    xfloat = embeddings.astype(F32)
    row_norm = jnp.sqrt(jnp.sum(xfloat * xfloat, axis=1, keepdims=True) + eps)
    unit = xfloat / row_norm
    xhat = lax.all_gather(unit.astype(BF16), DP_CLS, axis=0, tiled=True)
    labels = lax.all_gather(labels, "dp", axis=0, tiled=True)

    request, slot, column = plan_columns(sample_home[:, 0], sample_row, groups, group, shards, slots)
    incoming = lax.all_to_all(request.reshape(shards, slots), CLS, split_axis=0, concat_axis=0, tiled=True)
    incoming = incoming.reshape(-1)
    pick = (incoming[:, None] == jnp.arange(homes)[None, :]).astype(BF16)
    replies = matmul(pick, centres).astype(BF16)
    arrived = lax.all_to_all(
        replies.reshape(shards, slots, width), CLS, split_axis=0, concat_axis=0, tiled=True
    ).reshape(shards * slots, width)
    index = lax.all_gather(incoming, "dp", axis=0, tiled=True)

    place = (slot[:, None] == jnp.arange(shards * slots)[None, :]).astype(BF16)
    wfloat = matmul(place, arrived)
    col_norm = jnp.sqrt(jnp.sum(wfloat * wfloat, axis=1, keepdims=True) + eps)
    wunit = wfloat / col_norm
    what = wunit.astype(BF16)
    cosine = lax.dot_general(xhat, what, (((1,), (1,)), ((), ())), preferred_element_type=F32)
    target = ((labels - tile * columns)[:, None] == column[None, :]).astype(F32)
    exp_logit = jnp.exp(logit_scale * (cosine - margin * target))
    denominator = lax.psum(jnp.sum(exp_logit, axis=1), DP_CLS)
    grad_logit = (logit_scale * (exp_logit / denominator[:, None] - target)).astype(BF16)
    dwhat = lax.dot_general(grad_logit, xhat, (((0,), (0,)), ((), ())), preferred_element_type=F32)
    dfetched = (dwhat - wunit * jnp.sum(wunit * dwhat, axis=1, keepdims=True)) / col_norm
    packed = lax.dot_general(
        place, dfetched.astype(BF16), (((0,), (0,)), ((), ())), preferred_element_type=F32
    ).astype(BF16)
    received = lax.all_to_all(
        packed.reshape(shards, slots, width), CLS, split_axis=0, concat_axis=0, tiled=True
    ).reshape(shards * slots, width)
    returned = lax.all_gather(received, "dp", axis=0, tiled=True)
    dunit = lax.psum_scatter(matmul(grad_logit, what), DP_CLS, scatter_dimension=0, tiled=True)
    emb_grad = (dunit - unit * jnp.sum(unit * dunit, axis=1, keepdims=True)) / row_norm
    momentum_new, centres_new = update(index, returned, momentum, centres)
    return (emb_grad, momentum_new, centres_new)


def solution(mesh):
    torus = Mesh(mesh.devices.reshape(mesh.shape["dp"], 4, 4, 2), ("dp", "cls_0", "cls_1", "cls_2"))
    return jax.shard_map(
        body,
        mesh=torus,
        in_specs=(P(DP_CLS, None), P("dp"), P(CLS, None), P(CLS, None), P(CLS, None), P(CLS)),
        out_specs=(P(DP_CLS, None), P(CLS, None), P(CLS, None)),
        check_vma=False,
    )
```

time: 421 us -> 933 us (2.22)
  waiting for transfers between devices: 73.6 us -> 694 us
  local copies, waits for them, and re-layouts: 89.6 us -> 3.47 us
  other arithmetic: 87.3 us -> 22.7 us
  Pallas kernels: 0 us -> 22.2 us
  matrix products: 30 us -> 50 us
    reduce_scatter x0 -> x1, waiting for transfers between devices: none -> 645 us  [body(): lax.psum_scatter(matmul(grad_logit, what), DP_CLS, scatter_dimension=0, t...]
    all_to_all x5 -> x1, blocking collectives: 111 us -> 22.2 us  [body(): lax.all_to_all(packed.reshape(shards, slots, width), CLS, split_axis=0, c...]
    psum x0 -> x1, blocking collectives: none -> 63.6 us  [body(): denominator = lax.psum(jnp.sum(exp_logit, axis=1), DP_CLS)]
    gather x3 -> x0, local copies, waits for them, and re-layouts: 60.1 us -> none  [the longest x2 39.9 us: body(): fetched = arrived[home_shard, slot_rank]]
    all_to_all x3 -> x2, waiting for transfers between devices: 73.6 us -> 18.6 us  [the longest x1 18.6 us: body(): lax.all_to_all(replies.reshape(shards, slots, width), CLS, split_axis=0,...]
    scatter-add x1 -> x0, other arithmetic: 35 us -> none  [body(): centre_grad = jnp.zeros((home_rows, width), jnp.float32).at[incoming.resh...]
    all_gather x1 -> x2, waiting for transfers between devices: 0.01 us -> 30.6 us  [the longest x1 20.6 us: body(): returned = lax.all_gather(received, 'dp', axis=0, tiled=True)]
    all_gather x0 -> x2, blocking collectives: none -> 25.3 us  [the longest x1 13.4 us: body(): labels = lax.all_gather(labels, 'dp', axis=0, tiled=True)]
  transfers between devices with their start and end apart: 4 -> 5, of which waited for: 2 -> 4; matrix products, arithmetic and copies ran while one was open for 15% -> 3% of each run, Pallas kernels for 0% -> 2%
where the time goes in v1:
time: 933 us; the launch traced here: 932 us
  waiting for transfers between devices  694 us (74%)
  blocking collectives  111 us (12%)
  matrix products  50 us (5%)
  other arithmetic  22.7 us (2%)
  Pallas kernels  22.2 us (2%)
  starting transfers between devices  15 us (2%)
  between operations  13.9 us (1%)
    reduce_scatter x1, waiting for transfers between devices, body(): lax.psum_scatter(matmul(grad_logit, what), DP_CLS, scatter_dimension=0, t...  645 us
    psum x1, blocking collectives, body(): denominator = lax.psum(jnp.sum(exp_logit, axis=1), DP_CLS)  63.6 us
    dot_general x6, matrix products, matmul(): return jnp.dot(a, b, preferred_element_type=F32)  22.8 us
    all_to_all x1, blocking collectives, body(): lax.all_to_all(packed.reshape(shards, slots, width), CLS, split_axis=0, c...  22.2 us
    pallas_call x1, Pallas kernels, update(): pl.pallas_call(update_kernel, grid=(homes // rows,), in_specs=[pl.BlockSp...  22.2 us
    all_gather x1, waiting for transfers between devices, body(): returned = lax.all_gather(received, 'dp', axis=0, tiled=True)  20.6 us
  transfers between devices with their start and end apart: 5, of which 4 were waited for; matrix products, arithmetic and copies ran while one was open for 3% of the time, Pallas kernels for 2%

profile of v1, /device:TPU:0, one launch (start us, length us, event | category | flops | bytes accessed | tf_op | source)
XLA Modules:
  0.0 932.1 jit_solution(3857183475209621373)
XLA Ops:
  7.2 0.0 all-gather.3.cloned.1.call-start
  7.2 1.0 fusion.32
  8.2 1.6 fusion.79
  9.7 0.0 all-gather.3.cloned.1.call-update
  9.8 0.7 fusion.49
  10.5 0.8 convert_reduce_fusion
  11.4 0.1 select_reduce_fusion
  11.5 0.9 fusion.31
  12.3 0.8 multiply_reduce_fusion.2
  13.1 0.2 fusion.63
  13.3 1.1 fusion.19
  14.4 0.7 broadcast_select_fusion
  15.1 1.5 fusion.9
  16.6 0.7 convert_element_type.147
  17.3 7.4 all-to-all-start
  24.8 0.8 fusion.60
  25.6 13.4 %all_gather.13 = s32[8192]{0:T(1024)S(1)} all-gather(s32[2048]{0:T(1024)} %param.7), channel_id=1, replica_groups=mesh['dp'=4,'cls_0'=4,'cls_1'=4,'cls_2'=2] {'dp'}, dimensions={0}, use_global_device_ids=true | all-gather | bytes 40960 | tf_op jit(solution)/shard_map/all_gather | solution.py:118
  39.0 0.0 all-to-all-done
  39.0 0.5 broadcast.474
  39.5 0.7 reduce.10
  40.2 0.1 eq.147
  40.2 7.7 fusion.15
  47.9 7.3 all-to-all-start.1
  55.3 0.2 all-gather.5.cloned.1.call-start
  55.5 0.8 fusion.11
  56.4 18.6 %all-to-all-done.1 = bf16[32,32,512]{2,1,0:T(8,128)(2,1)S(1)} async-done(((bf16[32,32,512]{2,1,0:T(8,128)(2,1)}), bf16[32,32,512]{2,1,0:T(8,128)(2,1)S(1)}, u32[]{:S(2)}, u32[]{:S(2)}) %all-to-all-start.1) | async-done | bytes 1048608 | tf_op jit(solution)/shard_map/all_to_all | solution.py:125
  75.0 0.9 multiply_reduce_fusion.1
  75.9 10.0 %all-gather.3.cloned.1.call-done = bf16[8192,512]{1,0:T(8,128)(2,1)} async-done(((bf16[64,512]{1,0:T(8,128)(2,1)}), bf16[8192,512]{1,0:T(8,128)(2,1)}) %all-gather.3.cloned.1.call-update) | async-done | bytes 8388624 | tf_op jit(solution)/shard_map/all_gather | solution.py:117
  85.9 14.1 %fusion.7 = (f32[8192]{0:T(1024)S(1)}, f32[8192,512]{0,1:T(8,128)}) fusion(s32[8192]{0:T(1024)S(1)} %broadcast_subtract_fusion, s32[512]{0:T(512)S(1)} %bitcast.73, bf16[8192,512]{1,0:T(8,128)(2,1)} %all-gather.3.cloned.1.call-done, f32[512,512]{0,1:T(8,128)S(1)} %get-tuple-element.16, f32[512]{0:T(512)S(1)} %add_sqrt_fusion), kind=kOutput, calls=%fused_computation.10 | convolution fusion | flops 4316454912 | bytes 26284032 | tf_op jit(solution)/shard_map/dot_general | solution.py:135
  100.1 63.6 %psum.7 = f32[8192]{0:T(1024)S(1)} all-reduce(f32[8192]{0:T(1024)S(1)} %get-tuple-element.17), channel_id=1, replica_groups=mesh['dp'=4,'cls_0'=4,'cls_1'=4,'cls_2'=2] {'dp','cls_0','cls_1','cls_2'}, use_global_device_ids=true, to_apply=%region_8.9 | all-reduce | flops 8192 | bytes 65536 | tf_op jit(solution)/shard_map/psum | solution.py:138
  163.7 11.7 %fusion.5 = bf16[8192,512]{0,1:T(8,128)(2,1)} fusion(f32[8192,512]{0,1:T(8,128)} %get-tuple-element.18, f32[8192]{0:T(1024)S(1)} %psum.7, s32[8192]{0:T(1024)S(1)} %broadcast_subtract_fusion, s32[512]{0:T(512)S(1)} %bitcast.74), kind=kLoop, calls=%fused_computation.7 | loop fusion | flops 37748736 | bytes 25233408 | tf_op jit(solution)/shard_map/convert_element_type | solution.py:139
  175.4 11.0 %multiply_reduce_fusion = (f32[512]{0:T(512)S(1)}, f32[512,512]{0,1:T(8,128)S(1)}) fusion(f32[512,512]{0,1:T(8,128)S(1)} %get-tuple-element.16, f32[512]{0:T(512)S(1)} %add_sqrt_fusion, bf16[8192,512]{0,1:T(8,128)(2,1)} %fusion.5, bf16[8192,512]{1,0:T(8,128)(2,1)} %all-gather.3.cloned.1.call-done), kind=kOutput, calls=%fused_computation.29 | convolution fusion | flops 4295753216 | bytes 18878464 | tf_op jit(solution)/shard_map/dot_general | solution.py:140
  186.4 0.9 convolution_convert_fusion
  187.4 22.2 %all_to_all.16 = bf16[32,32,512]{2,1,0:T(8,128)(2,1)} all-to-all(bf16[32,32,512]{2,1,0:T(8,128)(2,1)S(1)} %bitcast.65), channel_id=1, replica_groups=mesh['dp'=4,'cls_0'=4,'cls_1'=4,'cls_2'=2] {'cls_0','cls_1','cls_2'}, dimensions={0} | all-to-all | bytes 2097152 | tf_op jit(solution)/shard_map/all_to_all | solution.py:145
  209.6 0.0 all-gather.5.cloned.1.call-update
  209.6 0.0 reduce-scatter.2.cloned.1.call-start
  209.6 11.7 %fusion.25 = f32[8192,512]{1,0:T(8,128)} fusion(bf16[8192,512]{0,1:T(8,128)(2,1)} %fusion.5, f32[512,512]{0,1:T(8,128)S(1)} %get-tuple-element.16, f32[512]{0:T(512)S(1)} %add_sqrt_fusion), kind=kOutput, calls=%fused_computation.37 | convolution fusion | flops 4295491584 | bytes 26216448 | tf_op jit(solution)/shard_map/dot_general | solution.py:25
  221.4 0.0 reduce-scatter.2.cloned.1.call-update
  221.4 12.0 %all_gather.14 = s32[4096]{0:T(1024)S(1)} all-gather(s32[1024]{0:T(1024)S(1)} %eq.147), channel_id=1, replica_groups=mesh['dp'=4,'cls_0'=4,'cls_1'=4,'cls_2'=2] {'dp'}, dimensions={0}, use_global_device_ids=true | all-gather | bytes 20480 | tf_op jit(solution)/shard_map/all_gather | solution.py:128
  233.3 20.6 %all-gather.5.cloned.1.call-done.returned_ref = bf16[4096,512]{1,0:T(8,128)(2,1)} async-done(((bf16[1024,512]{1,0:T(8,128)(2,1)}), bf16[4096,512]{1,0:T(8,128)(2,1)}) %all-gather.5.cloned.1.call-update) | async-done | bytes 4194320 | tf_op jit(solution)/shard_map/all_gather | solution.py:148
  254.0 0.0 copy-start
  254.0 2.2 copy-done
  256.2 0.0 copy-start.1
  256.2 22.2 %update.1 = (f32[4096,512]{1,0:T(8,128)}, bf16[4096,512]{1,0:T(8,128)(2,1)}) custom-call(s32[1,4096]{1,0:T(1,128)S(1)} %bitcast.62, bf16[4096,512]{1,0:T(8,128)(2,1)S(1)} %copy-done, f32[4096,512]{1,0:T(8,128)} %momentum_ref.1, bf16[4096,512]{1,0:T(8,128)(2,1)} %centres_ref.1), custom_call_target="tpu_custom_call" | custom-call | flops 17179869184 | bytes 33554432 | tf_op jit(solution)/shard_map/update/pallas_call | solution.py:82
  278.3 644.5 %reduce-scatter.2.cloned.1.call-done = f32[64,512]{1,0:T(8,128)} async-done(((f32[8192,512]{1,0:T(8,128)}), f32[64,512]{1,0:T(8,128)}) %reduce-scatter.2.cloned.1.call-update) | async-done | bytes 131088 | tf_op jit(solution)/shard_map/reduce_scatter | solution.py:149
  922.8 0.0 copy-done.1
  922.8 1.1 multiply_reduce_fusion.3
  923.9 1.7 subtract_divide_fusion
  (14 shorter events, 0.2 us)
Async XLA Ops:
  7.2 78.8 %all-gather.3.cloned.1.call-start = ((), (), s32[]{:S(2)}) async-start(), calls=%async_computation.4 | async-start | bytes 8454144 | tf_op jit(solution)/shard_map/all_gather | solution.py:117
  17.3 21.6 %all-to-all-start = ((s32[32,1,32]{2,1,0:T(1,128)}), s32[32,1,32]{2,1,0:T(1,128)S(1)}, u32[]{:S(2)}, u32[]{:S(2)}) async-start(s32[32,1,32]{2,1,0:T(1,128)} %bitcast.8), calls=%async_computation | async-start | bytes 32768 | tf_op jit(solution)/shard_map/all_to_all | solution.py:121
  47.9 27.1 %all-to-all-start.1 = ((bf16[32,32,512]{2,1,0:T(8,128)(2,1)}), bf16[32,32,512]{2,1,0:T(8,128)(2,1)S(1)}, u32[]{:S(2)}, u32[]{:S(2)}) async-start(bf16[32,32,512]{2,1,0:T(8,128)(2,1)} %bitcast.9), calls=%async_computation.1 | async-start | bytes 2097152 | tf_op jit(solution)/shard_map/all_to_all | solution.py:125
  55.3 198.7 %all-gather.5.cloned.1.call-start = ((), (), s32[]{:S(2)}) async-start(), calls=%async_computation.6 | async-start | bytes 5242880 | tf_op jit(solution)/shard_map/all_gather | solution.py:148
  209.6 713.2 %reduce-scatter.2.cloned.1.call-start = ((), (), s32[]{:S(2)}) async-start(), calls=%async_computation.5 | async-start | bytes 16908288 | tf_op jit(solution)/shard_map/reduce_scatter | solution.py:149
  254.0 2.2 copy-start
  256.2 666.7 %copy-start.1 = (bf16[64,512]{1,0:T(8,128)(2,1)S(1)}, bf16[64,512]{1,0:T(8,128)(2,1)}, u32[]{:S(2)}) copy-start(bf16[64,512]{1,0:T(8,128)(2,1)} %param.6) | copy-start | bytes 196612
Sparse Core Ops, SparseCore 0:
  11.6 74.3 all-gather.2
  209.7 44.2 all-gather.4
  256.4 666.4 reduce-scatter.1

commit v2 on v1

--- a/solution.py
+++ b/solution.py
@@ -101,6 +101,459 @@
     )(index.reshape(1, slots), returned, momentum, centres)
 
 
+MESH = pl.DeviceIdType.MESH
+N_TILES = 32
+ACROSS = 4
+
+
+def where_am_i():
+    z, y, x, c = (lax.axis_index(name) for name in DP_CLS)
+    return z, y, x, c, y * 8 + x * 2 + c
+
+
+def ahead(position, k):
+    return lax.rem(position + k, ACROSS)
+
+
+def tile_device(z, t):
+    return (z, lax.div(t, 8), lax.rem(lax.div(t, 2), ACROSS), lax.rem(t, 2))
+
+
+def remote(src, dst, send, recv, device):
+    return pltpu.make_async_remote_copy(
+        src_ref=src, dst_ref=dst, send_sem=send, recv_sem=recv, device_id=device, device_id_type=MESH
+    )
+
+
+def greet(devices, tiles=None):
+    barrier = pltpu.get_barrier_semaphore()
+    for device in devices:
+        pl.semaphore_signal(barrier, inc=1, device_id=device, device_id_type=MESH)
+    count = len(devices)
+    if tiles is not None:
+        z, me = tiles
+
+        @pl.loop(1, N_TILES)
+        def _(k):
+            pl.semaphore_signal(
+                barrier, inc=1, device_id=tile_device(z, lax.rem(me + k, N_TILES)), device_id_type=MESH
+            )
+
+        count += N_TILES - 1
+    pl.semaphore_wait(barrier, count)
+
+
+def fetch_kernel(
+    request_ref, labels_ref, centres_ref, slot_ref, fetched_out, index_out, labels_out,
+    incoming, index_all, labels_all, replies, arrived,
+    request_sent, request_came, reply_sent, reply_came, index_sent, index_came, labels_sent, labels_came,
+):
+    z, y, x, c, me = where_am_i()
+    homes = centres_ref.shape[0]
+    slots = replies.shape[1]
+    greet([(ahead(z, k), y, x, c) for k in range(1, ACROSS)], (z, me))
+
+    def ask(k):
+        t = lax.rem(me + k, N_TILES)
+        return remote(
+            request_ref.at[t], incoming.at[me], request_sent.at[t], request_came.at[me], tile_device(z, t)
+        )
+
+    def answer(t):
+        return remote(replies.at[t], arrived.at[me], reply_sent.at[t], reply_came.at[me], tile_device(z, t))
+
+    def answered(t):
+        return remote(replies.at[t], arrived.at[t], reply_sent.at[t], reply_came.at[t], tile_device(z, t))
+
+    def asked(t):
+        return remote(request_ref.at[t], incoming.at[t], request_sent.at[t], request_came.at[t], tile_device(z, t))
+
+    @pl.loop(1, N_TILES)
+    def _(k):
+        ask(k).start()
+
+    tell = [
+        remote(labels_ref, labels_all.at[k], labels_sent.at[k], labels_came.at[k], (ahead(z, k + 1), y, x, c))
+        for k in range(ACROSS - 1)
+    ]
+    for copy in tell:
+        copy.start()
+    incoming[me] = request_ref[me]
+
+    @pl.loop(1, N_TILES)
+    def _(k):
+        asked(lax.rem(me + k, N_TILES)).wait_recv()
+
+    share = [
+        remote(incoming, index_all.at[k], index_sent.at[k], index_came.at[k], (ahead(z, k + 1), y, x, c))
+        for k in range(ACROSS - 1)
+    ]
+    for copy in share:
+        copy.start()
+    row_ids = lax.broadcasted_iota(jnp.int32, (slots, homes), 1)
+    for q in (1, 2, 3, 0):
+        first = ahead(y, q) * 8
+        wanted = incoming[pl.ds(first, 8)].reshape(8, 128).T
+        pick = jnp.concatenate(
+            [jnp.where(row_ids == wanted[:slots, j : j + 1], 1.0, 0.0).astype(BF16) for j in range(8)], axis=0
+        )
+        found = jnp.dot(pick, centres_ref[...], preferred_element_type=F32).astype(BF16)
+        replies[pl.ds(first, 8)] = found.reshape(8, slots, found.shape[1])
+        for j in range(8):
+            if q:
+                answer(first + j).start()
+            else:
+
+                @pl.when(first + j != me)
+                def _(t=first + j):
+                    answer(t).start()
+
+    arrived[me] = replies[me]
+    index_out[z] = incoming[...]
+    labels_out[z] = labels_ref[...]
+    for k in range(ACROSS - 1):
+        source = ahead(z, ACROSS - 1 - k)
+        tell[k].wait()
+        labels_out[source] = labels_all[k]
+        share[k].wait()
+        index_out[source] = index_all[k]
+
+    @pl.loop(1, N_TILES)
+    def _(k):
+        answered(lax.rem(me + k, N_TILES)).wait_recv()
+
+    kept = slot_ref.shape[0]
+    place = slot_ref[...] == lax.broadcasted_iota(jnp.int32, (kept, N_TILES * slots), 1)
+    place = jnp.where(place, 1.0, 0.0).astype(BF16)
+    rows = arrived[...].reshape(N_TILES * slots, arrived.shape[2])
+    fetched_out[...] = jnp.dot(place, rows, preferred_element_type=F32).astype(BF16)
+
+    @pl.loop(1, N_TILES)
+    def _(k):
+        ask(k).wait_send()
+        answer(lax.rem(me + k, N_TILES)).wait_send()
+
+
+def fetch(request, labels, centres, slot, slots):
+    kept, width = slot.shape[0], centres.shape[1]
+    vmem = pl.BlockSpec(memory_space=pltpu.VMEM)
+    return pl.pallas_call(
+        fetch_kernel,
+        in_specs=[vmem] * 4,
+        out_specs=[vmem] * 3,
+        out_shape=[
+            jax.ShapeDtypeStruct((kept, width), BF16),
+            jax.ShapeDtypeStruct((ACROSS, N_TILES, 1, 128), jnp.int32),
+            jax.ShapeDtypeStruct((ACROSS, 16, 128), jnp.int32),
+        ],
+        scratch_shapes=[
+            pltpu.VMEM((N_TILES, 1, 128), jnp.int32),
+            pltpu.VMEM((ACROSS - 1, N_TILES, 1, 128), jnp.int32),
+            pltpu.VMEM((ACROSS - 1, 16, 128), jnp.int32),
+            pltpu.VMEM((N_TILES, slots, width), BF16),
+            pltpu.VMEM((N_TILES, slots, width), BF16),
+        ]
+        + [pltpu.SemaphoreType.DMA((N_TILES,))] * 4
+        + [pltpu.SemaphoreType.DMA((ACROSS - 1,))] * 4,
+        compiler_params=pltpu.CompilerParams(
+            collective_id=0, has_side_effects=True, vmem_limit_bytes=40 * 2**20
+        ),
+        name="fetch",
+    )(request, labels, centres, slot)
+
+
+def margin_kernel(
+    xhalf_ref, fetched_ref, labels_ref, column_ref, slot_ref, received_out, grad_out, turned_out,
+    xall, expo, den, got, inverse, acc, wunit, packed, arrived,
+    x_here, x_sent, x_came, den_sent, den_came, row_sent, row_came,
+):
+    z, y, x, c, me = where_am_i()
+    other = 1 - c
+    partner = (z, y, x, other)
+    along = {
+        "x": [(z, y, ahead(x, k), c) for k in range(1, ACROSS)],
+        "y": [(z, ahead(y, k), x, c) for k in range(1, ACROSS)],
+        "z": [(ahead(z, k), y, x, c) for k in range(1, ACROSS)],
+    }
+    greet(along["z"], (z, me))
+    pieces = 8
+    slots = packed.shape[1]
+
+    def piece_here(i):
+        two = pl.ds(2 * i, 2)
+        return pltpu.make_async_copy(xhalf_ref.at[:, two], xall.at[c, :, two], x_here.at[i])
+
+    def piece_over(i, slot):
+        two = pl.ds(2 * i, 2)
+        return remote(xhalf_ref.at[:, two], xall.at[slot, :, two], x_sent.at[i], x_came.at[i], partner)
+
+    @pl.loop(0, pieces)
+    def _(i):
+        piece_here(i).start()
+        piece_over(i, c).start()
+
+    wfloat = fetched_ref[...].astype(F32)
+    col_norm = jnp.sqrt(jnp.sum(wfloat * wfloat, axis=1, keepdims=True) + eps)
+    wunit[...] = wfloat / col_norm
+    turned_out[...] = wunit[...].T.astype(BF16)
+
+    def rows_of(side, i):
+        return jnp.concatenate([xall[side, g, 2 * i + j] for j in range(2) for g in range(ACROSS)], axis=0)
+
+    def exponents(side, i):
+        b = side * pieces + i
+        cosine = lax.dot_general(
+            wunit[...].astype(BF16), rows_of(side, i), (((1,), (1,)), ((), ())), preferred_element_type=F32
+        )
+        hit = column_ref[...] == labels_ref[pl.ds(b, 1)]
+        value = jnp.exp(logit_scale * jnp.where(hit, cosine - margin, cosine))
+        expo[b] = value
+        den[0, pl.ds(b, 1)] = jnp.sum(value, axis=0, keepdims=True)
+
+    @pl.loop(0, pieces)
+    def _(i):
+        piece_here(i).wait()
+        exponents(c, i)
+
+    @pl.loop(0, pieces)
+    def _(i):
+        piece_over(i, other).wait_recv()
+        exponents(other, i)
+
+    slot = 0
+    for stage, peers in enumerate(([partner], along["x"], along["y"], along["z"])):
+        copies = [
+            remote(den.at[stage], got.at[slot + k], den_sent.at[slot + k], den_came.at[slot + k], peer)
+            for k, peer in enumerate(peers)
+        ]
+        for copy in copies:
+            copy.start()
+        for copy in copies:
+            copy.wait()
+        total = den[stage]
+        for k in range(len(peers)):
+            total = total + got[slot + k]
+        if stage < 3:
+            den[stage + 1] = total
+        else:
+            inverse[...] = logit_scale / total
+        slot += len(peers)
+
+    acc[...] = jnp.zeros_like(acc)
+
+    @pl.loop(0, 2 * pieces)
+    def _(b):
+        hit = column_ref[...] == labels_ref[pl.ds(b, 1)]
+        share = expo[b] * inverse[pl.ds(b, 1)]
+        grad = jnp.where(hit, share - logit_scale, share).astype(BF16)
+        grad_out[b] = grad
+        acc[...] += jnp.dot(grad, rows_of(lax.div(b, pieces), lax.rem(b, pieces)), preferred_element_type=F32)
+
+    dwhat = acc[...]
+    unit = wunit[...]
+    wfloat = fetched_ref[...].astype(F32)
+    col_norm = jnp.sqrt(jnp.sum(wfloat * wfloat, axis=1, keepdims=True) + eps)
+    dfetched = ((dwhat - unit * jnp.sum(unit * dwhat, axis=1, keepdims=True)) / col_norm).astype(BF16)
+    kept = dfetched.shape[0]
+    place = slot_ref[...] == lax.broadcasted_iota(jnp.int32, (N_TILES * slots, kept), 0)
+    place = jnp.where(place, 1.0, 0.0).astype(BF16)
+    rows = jnp.dot(place, dfetched, preferred_element_type=F32).astype(BF16)
+    packed[...] = rows.reshape(packed.shape)
+
+    def give(t):
+        return remote(packed.at[t], arrived.at[me], row_sent.at[t], row_came.at[me], tile_device(z, t))
+
+    def given(t):
+        return remote(packed.at[t], arrived.at[t], row_sent.at[t], row_came.at[t], tile_device(z, t))
+
+    @pl.loop(1, N_TILES)
+    def _(k):
+        give(lax.rem(me + k, N_TILES)).start()
+
+    arrived[me] = packed[me]
+
+    @pl.loop(0, pieces)
+    def _(i):
+        piece_over(i, c).wait_send()
+
+    @pl.loop(1, N_TILES)
+    def _(k):
+        given(lax.rem(me + k, N_TILES)).wait_recv()
+
+    received_out[...] = arrived[...]
+
+    @pl.loop(1, N_TILES)
+    def _(k):
+        give(lax.rem(me + k, N_TILES)).wait_send()
+
+
+def margin_step(xhalf, fetched, labels, column, slot, slots):
+    kept, width = fetched.shape
+    blocks, block = labels.shape
+    vmem = pl.BlockSpec(memory_space=pltpu.VMEM)
+    return pl.pallas_call(
+        margin_kernel,
+        in_specs=[pl.BlockSpec(memory_space=pl.ANY)] + [vmem] * 4,
+        out_specs=[vmem] * 3,
+        out_shape=[
+            jax.ShapeDtypeStruct((N_TILES, slots, width), BF16),
+            jax.ShapeDtypeStruct((blocks, kept, block), BF16),
+            jax.ShapeDtypeStruct((width, kept), BF16),
+        ],
+        scratch_shapes=[
+            pltpu.VMEM((2, *xhalf.shape), BF16),
+            pltpu.VMEM((blocks, kept, block), F32),
+            pltpu.VMEM((4, blocks, block), F32),
+            pltpu.VMEM((10, blocks, block), F32),
+            pltpu.VMEM((blocks, block), F32),
+            pltpu.VMEM((kept, width), F32),
+            pltpu.VMEM((kept, width), F32),
+            pltpu.VMEM((N_TILES, slots, width), BF16),
+            pltpu.VMEM((N_TILES, slots, width), BF16),
+        ]
+        + [pltpu.SemaphoreType.DMA((8,))] * 3
+        + [pltpu.SemaphoreType.DMA((10,))] * 2
+        + [pltpu.SemaphoreType.DMA((N_TILES,))] * 2,
+        compiler_params=pltpu.CompilerParams(
+            collective_id=1, has_side_effects=True, vmem_limit_bytes=56 * 2**20
+        ),
+        name="margin_step",
+    )(xhalf, fetched, labels, column, slot)
+
+
+def reduce_kernel(
+    grad_ref, turned_ref, dunit_out, over, came, mine, first_a, first_b, next_a, next_b, second_a, second_b, last, third,
+    over_sent, over_came, step_sent, step_came,
+):
+    z, y, x, c, _ = where_am_i()
+    other = 1 - c
+    along_x = [(z, y, ahead(x, k), c) for k in range(1, ACROSS)]
+    along_y = [(z, ahead(y, k), x, c) for k in range(1, ACROSS)]
+    along_z = [(ahead(z, k), y, x, c) for k in range(1, ACROSS)]
+    partner = (z, y, x, other)
+    greet([partner] + along_x + along_y + along_z)
+    pieces = 8
+    half = mine.shape[2] // 2
+    low, high = pl.ds(0, half), pl.ds(half, half)
+    others = range(ACROSS - 1)
+
+    def product(side, i):
+        return jnp.dot(turned_ref[...], grad_ref[side * pieces + i], preferred_element_type=F32)
+
+    def hand_over(i):
+        two = pl.ds(2 * i, 2)
+        return remote(over.at[two], came.at[two], over_sent.at[i], over_came.at[i], partner)
+
+    @pl.loop(0, pieces)
+    def _(i):
+        part = product(other, i).astype(BF16)
+        over[2 * i] = part[:, : part.shape[1] // 2]
+        over[2 * i + 1] = part[:, part.shape[1] // 2 :]
+        hand_over(i).start()
+
+    @pl.loop(0, pieces)
+    def _(i):
+        part = product(c, i)
+        hand_over(i).wait_recv()
+        lanes = part.shape[1] // 2
+        row, column = lax.div(i, 2), 2 * lax.rem(i, 2)
+        mine[row, column] = (part[:, :lanes] + came[2 * i].astype(F32)).astype(BF16)
+        mine[row, column + 1] = (part[:, lanes:] + came[2 * i + 1].astype(F32)).astype(BF16)
+
+    def step(n, src, dst, device):
+        return remote(src, dst, step_sent.at[n], step_came.at[n], device)
+
+    one_a = [step(k, mine.at[:, ahead(x, k + 1), low], first_a.at[k], along_x[k]) for k in others]
+    one_b = [step(3 + k, mine.at[ahead(y, k + 1), :, high], first_b.at[k], along_y[k]) for k in others]
+    for copy in one_a + one_b:
+        copy.start()
+    for copy in one_a:
+        copy.wait_recv()
+
+    @pl.loop(0, ACROSS)
+    def _(i):
+        total = mine[i, x, low].astype(F32)
+        for k in others:
+            total = total + first_a[k, i].astype(F32)
+        next_a[i] = total.astype(BF16)
+
+    for copy in one_b:
+        copy.wait_recv()
+
+    @pl.loop(0, ACROSS)
+    def _(i):
+        total = mine[y, i, high].astype(F32)
+        for k in others:
+            total = total + first_b[k, i].astype(F32)
+        next_b[i] = total.astype(BF16)
+
+    two_a = [step(6 + k, next_a.at[ahead(y, k + 1)], second_a.at[k], along_y[k]) for k in others]
+    two_b = [step(9 + k, next_b.at[ahead(x, k + 1)], second_b.at[k], along_x[k]) for k in others]
+    for copy in two_a + two_b:
+        copy.start()
+    for copy in two_a + two_b:
+        copy.wait_recv()
+    top, bottom = next_a[y].astype(F32), next_b[x].astype(F32)
+    for k in others:
+        top = top + second_a[k].astype(F32)
+        bottom = bottom + second_b[k].astype(F32)
+    rows = last.shape[1]
+    last[:, :, :half] = top.T.astype(BF16).reshape(ACROSS, rows, half)
+    last[:, :, half:] = bottom.T.astype(BF16).reshape(ACROSS, rows, half)
+    three = [step(12 + k, last.at[ahead(z, k + 1)], third.at[k], along_z[k]) for k in others]
+    for copy in three:
+        copy.start()
+    for copy in three:
+        copy.wait_recv()
+    total = last[z].astype(F32)
+    for k in others:
+        total = total + third[k].astype(F32)
+    dunit_out[...] = total
+    for copy in one_a + one_b + two_a + two_b + three:
+        copy.wait_send()
+
+    @pl.loop(0, pieces)
+    def _(i):
+        hand_over(i).wait_send()
+
+
+def reduce_dunit(grad, turned, rows):
+    blocks, kept, block = grad.shape
+    width = turned.shape[0]
+    half, lanes = width // 2, block // 2
+    vmem = pl.BlockSpec(memory_space=pltpu.VMEM)
+    return pl.pallas_call(
+        reduce_kernel,
+        in_specs=[vmem] * 2,
+        out_specs=vmem,
+        out_shape=jax.ShapeDtypeStruct((rows, width), F32),
+        scratch_shapes=[
+            pltpu.VMEM((blocks, width, lanes), BF16),
+            pltpu.VMEM((blocks, width, lanes), BF16),
+            pltpu.VMEM((ACROSS, ACROSS, width, lanes), BF16),
+            pltpu.VMEM((3, ACROSS, half, lanes), BF16),
+            pltpu.VMEM((3, ACROSS, half, lanes), BF16),
+            pltpu.VMEM((ACROSS, half, lanes), BF16),
+            pltpu.VMEM((ACROSS, half, lanes), BF16),
+            pltpu.VMEM((3, half, lanes), BF16),
+            pltpu.VMEM((3, half, lanes), BF16),
+            pltpu.VMEM((ACROSS, rows, width), BF16),
+            pltpu.VMEM((3, rows, width), BF16),
+            pltpu.SemaphoreType.DMA((8,)),
+            pltpu.SemaphoreType.DMA((8,)),
+            pltpu.SemaphoreType.DMA((15,)),
+            pltpu.SemaphoreType.DMA((15,)),
+        ],
+        compiler_params=pltpu.CompilerParams(
+            collective_id=2, has_side_effects=True, vmem_limit_bytes=48 * 2**20
+        ),
+        cost_estimate=pl.CostEstimate(
+            flops=2 * blocks * block * kept * width, bytes_accessed=2**26, transcendentals=0
+        ),
+        name="reduce_dunit",
+    )(grad, turned)
+
+
 def body(embeddings, labels, centres, momentum, sample_home, sample_row):
     shards = lax.axis_size(CLS)
     groups = lax.axis_size("dp")
@@ -108,47 +561,24 @@
     tile = lax.axis_index(CLS)
     columns = sample_row.shape[0]
     slots = 2 * columns // shards // groups
-    width = embeddings.shape[1]
-    homes = centres.shape[0]
+    rows, width = embeddings.shape
 
     xfloat = embeddings.astype(F32)
     row_norm = jnp.sqrt(jnp.sum(xfloat * xfloat, axis=1, keepdims=True) + eps)
     unit = xfloat / row_norm
-    xhat = lax.all_gather(unit.astype(BF16), DP_CLS, axis=0, tiled=True)
-    labels = lax.all_gather(labels, "dp", axis=0, tiled=True)
+    xhalf = lax.all_gather(unit.astype(BF16), ("dp", "cls_0", "cls_1"), axis=0, tiled=True)
 
     request, slot, column = plan_columns(sample_home[:, 0], sample_row, groups, group, shards, slots)
-    incoming = lax.all_to_all(request.reshape(shards, slots), CLS, split_axis=0, concat_axis=0, tiled=True)
-    incoming = incoming.reshape(-1)
-    pick = (incoming[:, None] == jnp.arange(homes)[None, :]).astype(BF16)
-    replies = matmul(pick, centres).astype(BF16)
-    arrived = lax.all_to_all(
-        replies.reshape(shards, slots, width), CLS, split_axis=0, concat_axis=0, tiled=True
-    ).reshape(shards * slots, width)
-    index = lax.all_gather(incoming, "dp", axis=0, tiled=True)
-
-    place = (slot[:, None] == jnp.arange(shards * slots)[None, :]).astype(BF16)
-    wfloat = matmul(place, arrived)
-    col_norm = jnp.sqrt(jnp.sum(wfloat * wfloat, axis=1, keepdims=True) + eps)
-    wunit = wfloat / col_norm
-    what = wunit.astype(BF16)
-    cosine = lax.dot_general(xhat, what, (((1,), (1,)), ((), ())), preferred_element_type=F32)
-    target = ((labels - tile * columns)[:, None] == column[None, :]).astype(F32)
-    exp_logit = jnp.exp(logit_scale * (cosine - margin * target))
-    denominator = lax.psum(jnp.sum(exp_logit, axis=1), DP_CLS)
-    grad_logit = (logit_scale * (exp_logit / denominator[:, None] - target)).astype(BF16)
-    dwhat = lax.dot_general(grad_logit, xhat, (((0,), (0,)), ((), ())), preferred_element_type=F32)
-    dfetched = (dwhat - wunit * jnp.sum(wunit * dwhat, axis=1, keepdims=True)) / col_norm
-    packed = lax.dot_general(
-        place, dfetched.astype(BF16), (((0,), (0,)), ((), ())), preferred_element_type=F32
-    ).astype(BF16)
-    received = lax.all_to_all(
-        packed.reshape(shards, slots, width), CLS, split_axis=0, concat_axis=0, tiled=True
-    ).reshape(shards * slots, width)
-    returned = lax.all_gather(received, "dp", axis=0, tiled=True)
-    dunit = lax.psum_scatter(matmul(grad_logit, what), DP_CLS, scatter_dimension=0, tiled=True)
+    request = jnp.pad(request.reshape(shards, 1, slots), ((0, 0), (0, 0), (0, 128 - slots)))
+    fetched, index, labels = fetch(request, labels.reshape(16, 128), centres, slot[:, None], slots)
+    labels = labels.reshape(groups, 16, 2, rows).transpose(2, 1, 0, 3).reshape(16, -1) - tile * columns
+    received, grad, turned = margin_step(
+        xhalf.reshape(groups, 16, rows, width), fetched, labels, column[:, None], slot[None, :], slots
+    )
+    returned = lax.all_gather(received.reshape(shards * slots, width), "dp", axis=0, tiled=True)
+    dunit = reduce_dunit(grad, turned, rows)
     emb_grad = (dunit - unit * jnp.sum(unit * dunit, axis=1, keepdims=True)) / row_norm
-    momentum_new, centres_new = update(index, returned, momentum, centres)
+    momentum_new, centres_new = update(index[:, :, 0, :slots].reshape(-1), returned, momentum, centres)
     return (emb_grad, momentum_new, centres_new)
 
 

time: 933 us -> 231 us (0.25)
  waiting for transfers between devices: 694 us -> 37.3 us
  Pallas kernels: 22.2 us -> 158 us
  blocking collectives: 111 us -> 0 us
  matrix products: 50 us -> 3.5 us
  starting transfers between devices: 15 us -> 0.08 us
  other arithmetic: 22.7 us -> 9.42 us
    reduce_scatter x1 -> x0, waiting for transfers between devices: 645 us -> none  [body(): lax.psum_scatter(matmul(grad_logit, what), DP_CLS, scatter_dimension=0, t...]
    pallas_call x0 -> x3, Pallas kernels: none -> 136 us  [the longest x1 54.2 us: margin_step(): pl.pallas_call(margin_kernel, in_specs=[pl.BlockSpec(memory_space=pl.ANY)...]
    psum x1 -> x0, blocking collectives: 63.6 us -> none  [body(): denominator = lax.psum(jnp.sum(exp_logit, axis=1), DP_CLS)]
    dot_general x3 -> x0, matrix products: 26.1 us -> none  [the longest x1 14.1 us: body(): lax.dot_general(xhat, what, (((1,), (1,)), ((), ())), preferred_element_t...]
    all_gather x2 -> x0, blocking collectives: 25.3 us -> none  [the longest x1 13.4 us: body(): labels = lax.all_gather(labels, 'dp', axis=0, tiled=True)]
    all_to_all x1 -> x0, blocking collectives: 22.2 us -> none  [body(): lax.all_to_all(packed.reshape(shards, slots, width), CLS, split_axis=0, c...]
    dot_general x6 -> x3, matrix products: 22.8 us -> 2.44 us  [matmul(): return jnp.dot(a, b, preferred_element_type=F32)]
    all_to_all x2 -> x0, waiting for transfers between devices: 18.6 us -> none  [the longest x1 18.6 us: body(): lax.all_to_all(replies.reshape(shards, slots, width), CLS, split_axis=0,...]
  transfers between devices with their start and end apart: 5 -> 2, of which waited for: 4 -> 1; matrix products, arithmetic and copies ran while one was open for 3% -> 5% of each run, Pallas kernels for 2% -> 35%
where the time goes in v2:
time: 231 us; the launch traced here: 230 us
  Pallas kernels  158 us (68%)
  waiting for transfers between devices  37.3 us (16%)
  between operations  14.3 us (6%)
  other arithmetic  9.42 us (4%)
  local copies, waits for them, and re-layouts  7.42 us (3%)
  matrix products  3.5 us (2%)
    pallas_call x1, Pallas kernels, margin_step(): pl.pallas_call(margin_kernel, in_specs=[pl.BlockSpec(memory_space=pl.ANY)...  54.2 us
    pallas_call x1, Pallas kernels, reduce_dunit(): pl.pallas_call(reduce_kernel, in_specs=[vmem] * 2, out_specs=vmem, out_sh...  52.4 us
    all_gather x1, waiting for transfers between devices, body(): lax.all_gather(unit.astype(BF16), ('dp', 'cls_0', 'cls_1'), axis=0, tiled...  37.3 us
    pallas_call x1, Pallas kernels, fetch(): pl.pallas_call(fetch_kernel, in_specs=[vmem] * 4, out_specs=[vmem] * 3, o...  29.1 us
    pallas_call x1, Pallas kernels, update(): pl.pallas_call(update_kernel, grid=(homes // rows,), in_specs=[pl.BlockSp...  22.1 us
    unnamed x14, local copies, waits for them, and re-layouts  6.21 us
  transfers between devices with their start and end apart: 2, of which 1 were waited for; matrix products, arithmetic and copies ran while one was open for 5% of the time, Pallas kernels for 35%

profile of v2, /device:TPU:0, one launch (start us, length us, event | category | flops | bytes accessed | tf_op | source)
XLA Modules:
  0.0 229.9 jit_solution(3723224222992368867)
XLA Ops:
  7.2 0.0 copy-start.6
  7.2 0.0 copy-start.2
  7.2 0.0 all-gather.3.cloned.1.call-start
  7.2 1.0 fusion.13
  8.2 1.6 fusion.58
  9.8 0.0 all-gather.3.cloned.1.call-update
  9.8 0.0 all-gather.5.cloned.1.call-start
  9.8 0.8 convert_reduce_fusion
  10.7 0.1 select_reduce_fusion
  10.8 0.8 multiply_reduce_fusion
  11.6 0.8 fusion.12
  12.5 0.2 fusion.44
  12.7 1.1 fusion.7
  13.8 0.7 fusion.30
  14.5 0.7 broadcast_select_fusion
  15.2 1.5 fusion
  16.7 0.1 convert_element_type.127
  16.9 0.0 copy-done.6
  16.9 0.1 fusion.41
  17.0 0.8 fusion.2
  17.8 0.8 fusion.59
  18.6 0.0 copy-done.2
  18.6 0.0 copy-start
  18.6 2.2 copy-done
  20.8 29.1 %fetch.1 = (bf16[512,512]{1,0:T(8,128)(2,1)S(1)}, s32[4,32,1,128]{3,2,1,0:T(1,128)S(1)}, s32[4,16,128]{2,1,0:T(8,128)S(1)}) custom-call(s32[32,1,128]{2,1,0:T(1,128)S(1)} %pad.4.request_ref, s32[16,128]{1,0:T(8,128)S(1)} %bitcast.55, bf16[4096,512]{1,0:T(8,128)(2,1)S(1)} %copy-done, s32[512,1]{1,0:T(8,128)S(1)} %get-tuple-element.20.slot_ref), custom_call_target="tpu_custom_call" | custom-call | tf_op jit(solution)/shard_map/fetch/pallas_call | solution.py:240
  49.9 0.0 copy-start.1
  50.0 0.8 copy-done.1
  50.7 0.1 sub.84
  50.9 0.7 sub.86.labels_ref
  51.6 0.9 fusion.8.column_ref
  52.5 37.3 %all-gather.3.cloned.1.call-done = bf16[4096,512]{1,0:T(8,128)(2,1)} async-done(((bf16[64,512]{1,0:T(8,128)(2,1)}), bf16[4096,512]{1,0:T(8,128)(2,1)}) %all-gather.3.cloned.1.call-update) | async-done | bytes 4194320 | tf_op jit(solution)/shard_map/all_gather | solution.py:569
  89.8 54.2 %margin_step.1 = (bf16[32,32,512]{2,1,0:T(8,128)(2,1)}, bf16[16,512,512]{2,1,0:T(8,128)(2,1)}, bf16[512,512]{1,0:T(8,128)(2,1)}) custom-call(bf16[4,16,64,512]{3,2,1,0:T(8,128)(2,1)} %bitcast.56, bf16[512,512]{1,0:T(8,128)(2,1)} %copy-done.1, s32[16,512]{1,0:T(8,128)} %sub.86.labels_ref, s32[512,1]{1,0:T(8,128)} %fusion.8.column_ref, s32[1,512]{1,0:T(1,128)} %bitcast.66), custom_call_target="tpu_custom_call" | custom-call | tf_op jit(solution)/shard_map/margin_step/pallas_call | solution.py:394
  144.1 0.0 all-gather.5.cloned.1.call-update
  144.1 0.2 slice_reduce_fusion
  144.3 0.1 reshape_reshape_squeeze.3.index_ref
  144.4 0.0 copy-start.4
  144.4 1.0 copy-done.4
  145.4 0.0 copy-start.5
  145.4 52.4 %reduce_dunit.1 = f32[64,512]{1,0:T(8,128)S(1)} custom-call(bf16[16,512,512]{2,1,0:T(8,128)(2,1)} %get-tuple-element.13.grad_ref, bf16[512,512]{1,0:T(8,128)(2,1)S(1)} %copy-done.4), custom_call_target="tpu_custom_call" | custom-call | flops 4294967296 | bytes 67108864 | tf_op jit(solution)/shard_map/reduce_dunit/pallas_call | solution.py:525
  197.8 0.0 copy-done.5
  197.8 0.2 multiply_reduce_fusion.1
  198.0 0.8 subtract_divide_fusion
  198.8 0.0 all-gather.5.cloned.1.call-done.returned_ref
  198.8 0.0 copy-start.3
  198.8 2.2 copy-done.3
  200.9 22.1 %update.1 = (f32[4096,512]{1,0:T(8,128)}, bf16[4096,512]{1,0:T(8,128)(2,1)}) custom-call(s32[1,4096]{1,0:T(1,128)S(1)} %reshape_reshape_squeeze.3.index_ref, bf16[4096,512]{1,0:T(8,128)(2,1)S(1)} %copy-done.3, f32[4096,512]{1,0:T(8,128)} %momentum_ref.1, bf16[4096,512]{1,0:T(8,128)(2,1)} %centres_ref.3), custom_call_target="tpu_custom_call" | custom-call | flops 17179869184 | bytes 33554432 | tf_op jit(solution)/shard_map/update/pallas_call | solution.py:82
  (14 shorter events, 0.2 us)
Async XLA Ops:
  7.2 9.7 %copy-start.6 = (s32[2048,1]{0,1:T(1,128)S(1)}, s32[2048,1]{0,1:T(1,128)}, u32[]{:S(2)}) copy-start(s32[2048,1]{0,1:T(1,128)} %param.10) | copy-start | bytes 24580
  7.2 11.4 %copy-start.2 = (s32[2048]{0:T(1024)S(1)}, s32[2048]{0:T(1024)}, u32[]{:S(2)}) copy-start(s32[2048]{0:T(1024)} %param.7) | copy-start | bytes 24580
  7.2 82.6 %all-gather.3.cloned.1.call-start = ((), (), s32[]{:S(2)}) async-start(), calls=%async_computation | async-start | bytes 4259840 | tf_op jit(solution)/shard_map/all_gather | solution.py:569
  9.8 189.0 %all-gather.5.cloned.1.call-start = ((), (), s32[]{:S(2)}) async-start(), calls=%async_computation.1 | async-start | bytes 5242880 | tf_op jit(solution)/shard_map/all_gather | solution.py:578
  18.6 2.2 copy-start
  49.9 0.8 copy-start.1
  144.4 1.0 copy-start.4
  145.4 52.4 %copy-start.5 = (bf16[64,512]{1,0:T(8,128)(2,1)S(1)}, bf16[64,512]{1,0:T(8,128)(2,1)}, u32[]{:S(2)}) copy-start(bf16[64,512]{1,0:T(8,128)(2,1)} %param.6) | copy-start | bytes 196612
  198.8 2.2 copy-start.3
Sparse Core Ops, SparseCore 0:
  11.5 78.2 all-gather.2
  144.2 46.8 all-gather.4

commit v3 on v2

v3 whole, which is shorter than its diff:
```python
import jax
import jax.numpy as jnp
from jax import lax
from jax.experimental import pallas as pl
from jax.experimental.pallas import tpu as pltpu
from jax.sharding import Mesh
from jax.sharding import PartitionSpec as P

CLS = ("cls_0", "cls_1", "cls_2")
DP_CLS = ("dp", "cls_0", "cls_1", "cls_2")

eps = 1e-06
logit_scale = 64.0
margin = 0.35
momentum_rate = 0.9
learn_rate = 0.1
weight_decay = 0.0005
BF16 = jnp.bfloat16
F32 = jnp.float32


MESH = pl.DeviceIdType.MESH
N_TILES = 32
ACROSS = 4


def where_am_i():
    z, y, x, c = (lax.axis_index(name) for name in DP_CLS)
    return z, y, x, c, y * 8 + x * 2 + c


def ahead(position, k):
    return lax.rem(position + k, ACROSS)


def tile_device(z, t):
    return (z, lax.div(t, 8), lax.rem(lax.div(t, 2), ACROSS), lax.rem(t, 2))


def remote(src, dst, send, recv, device):
    return pltpu.make_async_remote_copy(
        src_ref=src, dst_ref=dst, send_sem=send, recv_sem=recv, device_id=device, device_id_type=MESH
    )


def greet(devices, tiles=None):
    barrier = pltpu.get_barrier_semaphore()
    for device in devices:
        pl.semaphore_signal(barrier, inc=1, device_id=device, device_id_type=MESH)
    count = len(devices)
    if tiles is not None:
        z, me = tiles

        @pl.loop(1, N_TILES)
        def _(k):
            pl.semaphore_signal(
                barrier, inc=1, device_id=tile_device(z, lax.rem(me + k, N_TILES)), device_id_type=MESH
            )

        count += N_TILES - 1
    pl.semaphore_wait(barrier, count)


def by_lanes(a, b):
    return lax.dot_general(a, b, (((1,), (1,)), ((), ())), preferred_element_type=F32)


def flag(condition):
    return jnp.where(condition, 1.0, 0.0)


def iota(shape, dim):
    return lax.broadcasted_iota(jnp.int32, shape, dim)


def plan_columns(home, row, group, slots):
    columns = home.shape[1]
    block = 128
    cuts = [slice(b * block, (b + 1) * block) for b in range(columns // block)]
    at_home = flag(iota((N_TILES, columns), 0) == home)
    upper = flag(iota((block, block), 0) < iota((block, block), 1)).astype(BF16)
    stacked = jnp.concatenate([at_home[:, cut] for cut in cuts], axis=0).astype(BF16)
    within = jnp.dot(stacked, upper, preferred_element_type=F32)
    before = [jnp.zeros((N_TILES, 1), F32)]
    for cut in cuts:
        before.append(before[-1] + jnp.sum(at_home[:, cut], axis=1, keepdims=True))
    count = jnp.broadcast_to(before[-1], (N_TILES, block)).astype(BF16)
    lower = flag(iota((N_TILES, N_TILES), 1) < iota((N_TILES, N_TILES), 0)).astype(BF16)
    offset = jnp.dot(lower, count, preferred_element_type=F32)
    first = ((offset.astype(jnp.int32) + (ACROSS - 1 - group)) >> 2).astype(F32)
    places, starts = [], []
    for b, cut in enumerate(cuts):
        mark = at_home[:, cut]
        rank = within[b * N_TILES : (b + 1) * N_TILES] + before[b] + offset
        places.append(jnp.sum(mark * rank, axis=0, keepdims=True))
        starts.append(jnp.sum(mark * first, axis=0, keepdims=True))
    place = jnp.concatenate(places, axis=1).astype(jnp.int32)
    start = jnp.concatenate(starts, axis=1).astype(jnp.int32)
    mine = (place & 3) == group
    kept = place >> 2
    slot = kept - start
    by_slot = flag(mine & (iota((block, columns), 0) == slot)).astype(BF16)
    digits = [at_home * (row >> 6).astype(F32), at_home * (row & 63).astype(F32)]
    asked = by_lanes(jnp.concatenate(digits, axis=0).astype(BF16), by_slot)
    request = (asked[:N_TILES] * 64 + asked[N_TILES:]).astype(jnp.int32)
    by_kept = flag(mine & (iota((block, columns), 0) == (kept & 127))).astype(BF16)
    lane = iota((1, columns), 1)
    parts = []
    for value in (home, slot, lane >> 6, lane & 63):
        for a in range(ACROSS):
            parts.append(jnp.where((kept >> 7) == a, value.astype(F32), 0.0))
    found = by_lanes(jnp.concatenate(parts, axis=0).astype(BF16), by_kept)
    turned = jnp.concatenate([found, jnp.zeros((block - found.shape[0], block), F32)], axis=0).T
    runs = range(ACROSS)
    slot_row = jnp.concatenate([found[a : a + 1] * slots + found[4 + a : 5 + a] for a in runs], axis=1)
    slot_column = jnp.concatenate([turned[:, a : a + 1] * slots + turned[:, 4 + a : 5 + a] for a in runs], axis=0)
    column = jnp.concatenate([turned[:, 8 + a : 9 + a] * 64 + turned[:, 12 + a : 13 + a] for a in runs], axis=0)
    return request, slot_row.astype(jnp.int32), slot_column.astype(jnp.int32), column.astype(jnp.int32)


def fetch_kernel(
    emb_ref, home_ref, row_ref, labels_ref, centres_hbm,
    xhalf, fetched_out, column_out, slot_out, index_out, labels_out,
    xhat, centres, request, incoming, index_all, labels_all, replies, arrived,
    local_sem, request_sent, request_came, reply_sent, reply_came, index_sent, index_came, labels_sent, labels_came,
    phase_sent, phase_came,
):
    z, y, x, c, me = where_am_i()
    homes = centres.shape[0]
    slots = replies.shape[1]
    load = pltpu.make_async_copy(centres_hbm, centres, local_sem.at[0])
    load.start()
    xfloat = emb_ref[...].astype(F32)
    row_norm = jnp.sqrt(jnp.sum(xfloat * xfloat, axis=1, keepdims=True) + eps)
    xhat[...] = (xfloat / row_norm).astype(BF16)
    keep = pltpu.make_async_copy(xhat, xhalf.at[z, y, x], local_sem.at[1])
    keep.start()
    asked, slot_row, slot_column, column = plan_columns(home_ref[...], row_ref[...], z, slots)
    request[...] = asked.reshape(request.shape)
    slot_out[...] = slot_row
    column_out[...] = column
    greet([(ahead(z, k), y, x, c) for k in range(1, ACROSS)], (z, me))

    def along(axis, k):
        return {"x": (z, y, ahead(x, k), c), "y": (z, ahead(y, k), x, c), "z": (ahead(z, k), y, x, c)}[axis]

    def ask(k):
        t = lax.rem(me + k, N_TILES)
        return remote(request.at[t], incoming.at[me], request_sent.at[t], request_came.at[me], tile_device(z, t))

    def asked_by(t):
        return remote(request.at[t], incoming.at[t], request_sent.at[t], request_came.at[t], tile_device(z, t))

    def answer(t):
        return remote(replies.at[t], arrived.at[me], reply_sent.at[t], reply_came.at[me], tile_device(z, t))

    def answered(t):
        return remote(replies.at[t], arrived.at[t], reply_sent.at[t], reply_came.at[t], tile_device(z, t))

    @pl.loop(1, N_TILES)
    def _(k):
        ask(k).start()

    def spread(part, phase):
        first, size, axes = ((0, 16, "zxy"), (16, 16, "zyx"), (32, 32, "xyz"))[part]
        done = axes[:phase]
        if phase == 0:
            src = xhat.at[pl.ds(first, size)]
            dst = xhalf.at[z, y, x, pl.ds(first, size)]
        else:
            everything = pl.ds(0, ACROSS)
            where = [everything if a in done else p for a, p in zip("zyx", (z, y, x))]
            src = dst = xhalf.at[where[0], where[1], where[2], pl.ds(first, size)]
        copies = []
        for k in range(ACROSS - 1):
            n = (part * 3 + phase) * 3 + k
            copies.append(remote(src, dst, phase_sent.at[n], phase_came.at[n], along(axes[phase], k + 1)))
        return copies

    waves = [[spread(part, phase) for part in range(3)] for phase in range(3)]
    flying = []

    def send(copies):
        for copy in copies:
            copy.start()
        flying.extend(copies)

    def land(copies):
        for copy in copies:
            copy.wait_recv()

    tell = [
        remote(labels_ref, labels_all.at[k], labels_sent.at[k], labels_came.at[k], along("z", k + 1))
        for k in range(ACROSS - 1)
    ]
    send(waves[0][2])
    send(waves[0][0])
    send(waves[0][1])
    send(tell)
    incoming[me] = request[me]

    @pl.loop(1, N_TILES)
    def _(k):
        asked_by(lax.rem(me + k, N_TILES)).wait_recv()

    share = [
        remote(incoming, index_all.at[k], index_sent.at[k], index_came.at[k], along("z", k + 1))
        for k in range(ACROSS - 1)
    ]
    send(share)
    keep.wait()
    for part in (2, 0, 1):
        land(waves[0][part])
        send(waves[1][part])
    load.wait()
    row_ids = iota((slots, homes), 1)
    for q in (1, 2, 3, 0):
        first = ahead(y, q) * 8
        wanted = incoming[pl.ds(first, 8)].reshape(8, 128).T
        pick = jnp.concatenate(
            [flag(row_ids == wanted[:slots, j : j + 1]).astype(BF16) for j in range(8)], axis=0
        )
        found = jnp.dot(pick, centres[...], preferred_element_type=F32).astype(BF16)
        replies[pl.ds(first, 8)] = found.reshape(8, slots, found.shape[1])
        for j in range(8):
            if q:
                answer(first + j).start()
            else:

                @pl.when(first + j != me)
                def _(t=first + j):
                    answer(t).start()

        part = {1: 2, 2: 0, 3: 1}.get(q)
        if part is not None:
            land(waves[1][part])
            send(waves[2][part])

    arrived[me] = replies[me]
    index_out[z] = incoming[...]
    labels_out[z] = labels_ref[...]
    land(tell + share)
    for k in range(ACROSS - 1):
        source = ahead(z, ACROSS - 1 - k)
        labels_out[source] = labels_all[k]
        index_out[source] = index_all[k]

    @pl.loop(1, N_TILES)
    def _(k):
        answered(lax.rem(me + k, N_TILES)).wait_recv()

    kept = slot_column.shape[0]
    place = flag(slot_column == iota((kept, N_TILES * slots), 1)).astype(BF16)
    rows = arrived[...].reshape(N_TILES * slots, arrived.shape[2])
    fetched_out[...] = jnp.dot(place, rows, preferred_element_type=F32).astype(BF16)
    for part in (0, 1, 2):
        land(waves[2][part])
    for copy in flying:
        copy.wait_send()

    @pl.loop(1, N_TILES)
    def _(k):
        ask(k).wait_send()
        answer(lax.rem(me + k, N_TILES)).wait_send()


def fetch(embeddings, home, row, labels, centres, kept, slots):
    rows, width = embeddings.shape
    vmem, anywhere = pl.BlockSpec(memory_space=pltpu.VMEM), pl.BlockSpec(memory_space=pl.ANY)
    return pl.pallas_call(
        fetch_kernel,
        in_specs=[vmem] * 4 + [anywhere],
        out_specs=[anywhere] + [vmem] * 5,
        out_shape=[
            jax.ShapeDtypeStruct((ACROSS, ACROSS, ACROSS, rows, width), BF16),
            jax.ShapeDtypeStruct((kept, width), BF16),
            jax.ShapeDtypeStruct((kept, 1), jnp.int32),
            jax.ShapeDtypeStruct((1, kept), jnp.int32),
            jax.ShapeDtypeStruct((ACROSS, N_TILES, 1, 128), jnp.int32),
            jax.ShapeDtypeStruct((ACROSS, 16, 128), jnp.int32),
        ],
        scratch_shapes=[
            pltpu.VMEM((rows, width), BF16),
            pltpu.VMEM(centres.shape, BF16),
            pltpu.VMEM((N_TILES, 1, 128), jnp.int32),
            pltpu.VMEM((N_TILES, 1, 128), jnp.int32),
            pltpu.VMEM((ACROSS - 1, N_TILES, 1, 128), jnp.int32),
            pltpu.VMEM((ACROSS - 1, 16, 128), jnp.int32),
            pltpu.VMEM((N_TILES, slots, width), BF16),
            pltpu.VMEM((N_TILES, slots, width), BF16),
            pltpu.SemaphoreType.DMA((2,)),
        ]
        + [pltpu.SemaphoreType.DMA((N_TILES,))] * 4
        + [pltpu.SemaphoreType.DMA((ACROSS - 1,))] * 4
        + [pltpu.SemaphoreType.DMA((27,))] * 2,
        compiler_params=pltpu.CompilerParams(
            collective_id=0, has_side_effects=True, vmem_limit_bytes=40 * 2**20
        ),
        name="fetch",
    )(embeddings, home, row, labels, centres)


def margin_kernel(
    xhalf_ref, fetched_ref, labels_ref, column_ref, slot_ref, index_ref, emb_ref, grads_hbm, emb_out,
    xall, expo, den, got, inverse, acc, wunit, turned, packed, arrived, nearby,
    over, came, mine, first_a, first_b, next_a, next_b, second_a, second_b, last, third,
    x_here, x_sent, x_came, den_sent, den_came, row_sent, row_came, ring_sent, ring_came,
    over_sent, over_came, step_sent, step_came, out_sem,
):
    z, y, x, c, me = where_am_i()
    other = 1 - c
    partner = (z, y, x, other)
    others = range(ACROSS - 1)
    along_x = [(z, y, ahead(x, k + 1), c) for k in others]
    along_y = [(z, ahead(y, k + 1), x, c) for k in others]
    along_z = [(ahead(z, k + 1), y, x, c) for k in others]
    greet(along_z, (z, me))
    pieces = 8
    slots = packed.shape[1]

    def piece_here(i):
        two = pl.ds(2 * i, 2)
        return pltpu.make_async_copy(xhalf_ref.at[:, two], xall.at[c, :, two], x_here.at[i])

    def piece_over(i, slot):
        two = pl.ds(2 * i, 2)
        return remote(xhalf_ref.at[:, two], xall.at[slot, :, two], x_sent.at[i], x_came.at[i], partner)

    @pl.loop(0, pieces)
    def _(i):
        piece_over(i, c).start()
        piece_here(i).start()

    def column_norm():
        wfloat = fetched_ref[...].astype(F32)
        return wfloat, jnp.sqrt(jnp.sum(wfloat * wfloat, axis=1, keepdims=True) + eps)

    wfloat, col_norm = column_norm()
    wunit[...] = wfloat / col_norm
    turned[...] = wunit[...].T.astype(BF16)

    def rows_of(side, i):
        return jnp.concatenate([xall[side, g, 2 * i + j] for j in range(2) for g in range(ACROSS)], axis=0)

    def exponents(group, i):
        @pl.when(c == 0)
        def _():
            piece_here(i).wait()

        @pl.when(c == 1)
        def _():
            piece_over(i, other).wait_recv()

        for side in range(2):
            if side:

                @pl.when(c == 1)
                def _():
                    piece_here(i).wait()

                @pl.when(c == 0)
                def _():
                    piece_over(i, other).wait_recv()

            cosine = by_lanes(wunit[...].astype(BF16), rows_of(side, i))
            hit = column_ref[...] == labels_ref[pl.ds(side * pieces + i, 1)]
            value = jnp.exp(logit_scale * jnp.where(hit, cosine - margin, cosine))
            expo[side * pieces + i] = value
            den[group, 0, pl.ds(2 * (i - 4 * group) + side, 1)] = jnp.sum(value, axis=0, keepdims=True)

    stages = ((0, [partner]), (1, along_x), (4, along_y), (7, along_z))

    def stage_copies(group, stage):
        slot, peers = stages[stage]
        return [
            remote(
                den.at[group, stage],
                got.at[group, slot + k],
                den_sent.at[10 * group + slot + k],
                den_came.at[10 * group + slot + k],
                peer,
            )
            for k, peer in enumerate(peers)
        ]

    def stage_start(group, stage):
        for copy in stage_copies(group, stage):
            copy.start()

    def stage_end(group, stage):
        for copy in stage_copies(group, stage):
            copy.wait()
        slot, peers = stages[stage]
        total = den[group, stage]
        for k in range(len(peers)):
            total = total + got[group, slot + k]
        if stage < 3:
            den[group, stage + 1] = total
            stage_start(group, stage + 1)
        else:
            inverse[group] = logit_scale / total

    def gradients(group, i):
        for side in range(2):
            b = side * pieces + i
            hit = column_ref[...] == labels_ref[pl.ds(b, 1)]
            share = expo[b] * inverse[group, pl.ds(2 * (i - 4 * group) + side, 1)]
            grad = jnp.where(hit, share - logit_scale, share).astype(BF16)
            expo[b] = grad.astype(F32)
            acc[...] += jnp.dot(grad, rows_of(side, i), preferred_element_type=F32)

    acc[...] = jnp.zeros_like(acc)

    @pl.loop(0, 4)
    def _(i):
        exponents(0, i)

    stage_start(0, 0)
    for n in range(4):
        exponents(1, 4 + n)
        if n == 3:
            stage_start(1, 0)
        stage_end(0, n)
    for n in range(4):
        gradients(0, n)
        stage_end(1, n)

    @pl.loop(4, pieces)
    def _(i):
        gradients(1, i)

    dwhat = acc[...]
    unit = wunit[...]
    _, col_norm = column_norm()
    dfetched = ((dwhat - unit * jnp.sum(unit * dwhat, axis=1, keepdims=True)) / col_norm).astype(BF16)
    kept = dfetched.shape[0]
    place = flag(slot_ref[...] == iota((N_TILES * slots, kept), 0)).astype(BF16)
    packed[...] = jnp.dot(place, dfetched, preferred_element_type=F32).astype(BF16).reshape(packed.shape)

    def give(t):
        return remote(packed.at[t], arrived.at[me], row_sent.at[t], row_came.at[me], tile_device(z, t))

    def given(t):
        return remote(packed.at[t], arrived.at[t], row_sent.at[t], row_came.at[t], tile_device(z, t))

    @pl.loop(1, N_TILES)
    def _(k):
        give(lax.rem(me + k, N_TILES)).start()

    arrived[me] = packed[me]

    def tiles_of(n):
        return pl.ds(8 * ahead(y, n), 8)

    def down(n):
        return remote(
            arrived.at[tiles_of(n)], nearby.at[0, tiles_of(n)], ring_sent.at[n], ring_came.at[n], along_z[2]
        )

    def up(n):
        return remote(
            arrived.at[tiles_of(n)], nearby.at[1, tiles_of(n)], ring_sent.at[4 + n], ring_came.at[4 + n], along_z[0]
        )

    def onward(n):
        source, device = (1, along_z[0]) if n < 2 else (0, along_z[2])
        return remote(
            nearby.at[source, tiles_of(n)],
            nearby.at[2, tiles_of(n)],
            ring_sent.at[8 + n],
            ring_came.at[8 + n],
            device,
        )

    def pass_on(n):
        for j in range(8):
            t = 8 * ahead(y, n) + j
            if n:
                given(t).wait_recv()
            else:

                @pl.when(t != me)
                def _(t=t):
                    given(t).wait_recv()

        up(n).start()
        down(n).start()

    half = mine.shape[2] // 2
    low, high = pl.ds(0, half), pl.ds(half, half)

    def product(side, i):
        return jnp.dot(turned[...], expo[side * pieces + i].astype(BF16), preferred_element_type=F32)

    def hand_over(i):
        two = pl.ds(2 * i, 2)
        return remote(over.at[two], came.at[two], over_sent.at[i], over_came.at[i], partner)

    @pl.loop(0, pieces)
    def _(i):
        part = product(other, i).astype(BF16)
        over[2 * i] = part[:, : part.shape[1] // 2]
        over[2 * i + 1] = part[:, part.shape[1] // 2 :]
        hand_over(i).start()

    def own_part(i):
        part = product(c, i)
        hand_over(i).wait_recv()
        lanes = part.shape[1] // 2
        row, column = lax.div(i, 2), 2 * lax.rem(i, 2)
        mine[row, column] = (part[:, :lanes] + came[2 * i].astype(F32)).astype(BF16)
        mine[row, column + 1] = (part[:, lanes:] + came[2 * i + 1].astype(F32)).astype(BF16)

    pass_on(0)
    pl.loop(0, 4)(own_part)
    pass_on(1)
    pl.loop(4, 8)(own_part)
    pass_on(2)
    pass_on(3)

    def step(n, src, dst, device):
        return remote(src, dst, step_sent.at[n], step_came.at[n], device)

    one_a = [step(k, mine.at[:, ahead(x, k + 1), low], first_a.at[k], along_x[k]) for k in others]
    one_b = [step(3 + k, mine.at[ahead(y, k + 1), :, high], first_b.at[k], along_y[k]) for k in others]
    for copy in one_a + one_b:
        copy.start()

    block = expo.shape[1]

    def scatter(source, rows_ref, fresh):
        slot_rows = rows_ref.reshape(N_TILES * slots, rows_ref.shape[2])
        index = index_ref[source]

        @pl.loop(0, pieces)
        def _(r):
            pick = flag(iota((block, N_TILES * slots), 0) + r * block == index).astype(BF16)
            grad = jnp.dot(pick, slot_rows, preferred_element_type=F32)
            expo[r] = grad if fresh else expo[r] + grad

    scatter(z, arrived[...], True)
    for n in range(2):
        up(n).wait_recv()
        onward(n).start()
    for n in range(2, 4):
        down(n).wait_recv()
        onward(n).start()
    for n in range(2):
        down(n).wait_recv()
    scatter(ahead(z, 1), nearby[0], False)
    for n in range(2, 4):
        up(n).wait_recv()
    scatter(ahead(z, 3), nearby[1], False)
    for copy in one_a + one_b:
        copy.wait_recv()

    @pl.loop(0, ACROSS)
    def _(i):
        total, below = mine[i, x, low].astype(F32), mine[y, i, high].astype(F32)
        for k in others:
            total = total + first_a[k, i].astype(F32)
            below = below + first_b[k, i].astype(F32)
        next_a[i] = total.astype(BF16)
        next_b[i] = below.astype(BF16)

    two_a = [step(6 + k, next_a.at[ahead(y, k + 1)], second_a.at[k], along_y[k]) for k in others]
    two_b = [step(9 + k, next_b.at[ahead(x, k + 1)], second_b.at[k], along_x[k]) for k in others]
    for copy in two_a + two_b:
        copy.start()
    for n in range(4):
        onward(n).wait_recv()
    scatter(ahead(z, 2), nearby[2], False)
    save = [pltpu.make_async_copy(expo.at[pl.ds(0, pieces)], grads_hbm, out_sem.at[0])]
    save[0].start()
    for copy in two_a + two_b:
        copy.wait_recv()
    top, bottom = next_a[y].astype(F32), next_b[x].astype(F32)
    for k in others:
        top = top + second_a[k].astype(F32)
        bottom = bottom + second_b[k].astype(F32)
    rows = last.shape[1]
    last[:, :, :half] = top.T.astype(BF16).reshape(ACROSS, rows, half)
    last[:, :, half:] = bottom.T.astype(BF16).reshape(ACROSS, rows, half)
    three = [step(12 + k, last.at[ahead(z, k + 1)], third.at[k], along_z[k]) for k in others]
    for copy in three:
        copy.start()
    xfloat = emb_ref[...].astype(F32)
    row_norm = jnp.sqrt(jnp.sum(xfloat * xfloat, axis=1, keepdims=True) + eps)
    xunit = xfloat / row_norm
    for copy in three:
        copy.wait_recv()
    dunit = last[z].astype(F32)
    for k in others:
        dunit = dunit + third[k].astype(F32)
    emb_out[...] = (dunit - xunit * jnp.sum(xunit * dunit, axis=1, keepdims=True)) / row_norm
    for copy in one_a + one_b + two_a + two_b + three:
        copy.wait_send()
    for n in range(4):
        up(n).wait_send()
        down(n).wait_send()
        onward(n).wait_send()

    @pl.loop(0, pieces)
    def _(i):
        hand_over(i).wait_send()
        piece_over(i, c).wait_send()

    @pl.loop(1, N_TILES)
    def _(k):
        give(lax.rem(me + k, N_TILES)).wait_send()

    save[0].wait()


def margin_step(xhalf, fetched, labels, column, slot, index, embeddings, slots, homes):
    kept, width = fetched.shape
    blocks, block = labels.shape
    rows = embeddings.shape[0]
    half, lanes = width // 2, block // 2
    vmem, anywhere = pl.BlockSpec(memory_space=pltpu.VMEM), pl.BlockSpec(memory_space=pl.ANY)
    return pl.pallas_call(
        margin_kernel,
        in_specs=[anywhere] + [vmem] * 6,
        out_specs=[anywhere, vmem],
        out_shape=[
            jax.ShapeDtypeStruct((homes // block, block, width), F32),
            jax.ShapeDtypeStruct((rows, width), F32),
        ],
        scratch_shapes=[
            pltpu.VMEM((2, *xhalf.shape), BF16),
            pltpu.VMEM((blocks, kept, block), F32),
            pltpu.VMEM((2, 4, blocks // 2, block), F32),
            pltpu.VMEM((2, 10, blocks // 2, block), F32),
            pltpu.VMEM((2, blocks // 2, block), F32),
            pltpu.VMEM((kept, width), F32),
            pltpu.VMEM((kept, width), F32),
            pltpu.VMEM((width, kept), BF16),
            pltpu.VMEM((N_TILES, slots, width), BF16),
            pltpu.VMEM((N_TILES, slots, width), BF16),
            pltpu.VMEM((3, N_TILES, slots, width), BF16),
            pltpu.VMEM((blocks, width, lanes), BF16),
            pltpu.VMEM((blocks, width, lanes), BF16),
            pltpu.VMEM((ACROSS, ACROSS, width, lanes), BF16),
            pltpu.VMEM((3, ACROSS, half, lanes), BF16),
            pltpu.VMEM((3, ACROSS, half, lanes), BF16),
            pltpu.VMEM((ACROSS, half, lanes), BF16),
            pltpu.VMEM((ACROSS, half, lanes), BF16),
            pltpu.VMEM((3, half, lanes), BF16),
            pltpu.VMEM((3, half, lanes), BF16),
            pltpu.VMEM((ACROSS, rows, width), BF16),
            pltpu.VMEM((3, rows, width), BF16),
        ]
        + [pltpu.SemaphoreType.DMA((8,))] * 3
        + [pltpu.SemaphoreType.DMA((20,))] * 2
        + [pltpu.SemaphoreType.DMA((N_TILES,))] * 2
        + [pltpu.SemaphoreType.DMA((12,))] * 2
        + [pltpu.SemaphoreType.DMA((8,))] * 2
        + [pltpu.SemaphoreType.DMA((15,))] * 2
        + [pltpu.SemaphoreType.DMA((1,))],
        compiler_params=pltpu.CompilerParams(
            collective_id=1, has_side_effects=True, vmem_limit_bytes=60 * 2**20
        ),
        name="margin_step",
    )(xhalf, fetched, labels, column, slot, index, embeddings)


def body(embeddings, labels, centres, momentum, sample_home, sample_row):
    groups = lax.axis_size("dp")
    tile = lax.axis_index(CLS)
    columns = sample_row.shape[0]
    kept = columns // groups
    slots = 2 * kept // N_TILES
    rows, width = embeddings.shape
    homes = centres.shape[0]
    xhalf, fetched, column, slot, index, labels = fetch(
        embeddings,
        sample_home.reshape(1, columns),
        sample_row.reshape(1, columns),
        labels.reshape(16, 128),
        centres,
        kept,
        slots,
    )
    labels = labels.reshape(groups, 16, 2, rows).transpose(2, 1, 0, 3).reshape(16, -1) - tile * columns
    index = index[:, :, 0, :slots].reshape(groups, 1, N_TILES * slots)
    centre_grad, emb_grad = margin_step(
        xhalf.reshape(groups, 16, rows, width), fetched, labels, column, slot, index, embeddings, slots, homes
    )
    centre_float = centres.astype(F32)
    momentum_new = momentum_rate * momentum + centre_grad.reshape(homes, width) + weight_decay * centre_float
    centres_new = (centre_float - learn_rate * momentum_new).astype(BF16)
    return (emb_grad, momentum_new, centres_new)


def solution(mesh):
    torus = Mesh(mesh.devices.reshape(mesh.shape["dp"], 4, 4, 2), ("dp", "cls_0", "cls_1", "cls_2"))
    return jax.shard_map(
        body,
        mesh=torus,
        in_specs=(P(DP_CLS, None), P("dp"), P(CLS, None), P(CLS, None), P(CLS, None), P(CLS)),
        out_specs=(P(DP_CLS, None), P(CLS, None), P(CLS, None)),
        check_vma=False,
    )
```

time: 231 us -> 180 us (0.78)
  waiting for transfers between devices: 37.3 us -> 0 us
  between operations: 14.3 us -> 0.71 us
  local copies, waits for them, and re-layouts: 7.42 us -> 11.6 us
  matrix products: 3.5 us -> 0 us
  other arithmetic: 9.42 us -> 12.6 us
  Pallas kernels: 158 us -> 155 us
    all_gather x2 -> x0, waiting for transfers between devices: 37.3 us -> none  [the longest x1 37.3 us: body(): lax.all_gather(unit.astype(BF16), ('dp', 'cls_0', 'cls_1'), axis=0, tiled...]
    convert_element_type x7 -> x1, other arithmetic: 3.33 us -> 12.6 us  [body(): centres_new = (centre_float - learn_rate * momentum_new).astype(BF16)]
    reduce_sum x6 -> x0, other arithmetic: 3.72 us -> none  [the longest x1 0.95 us: body(): row_norm = jnp.sqrt(jnp.sum(xfloat * xfloat, axis=1, keepdims=True) + eps)]
    unnamed x14 -> x21, local copies, waits for them, and re-layouts: 6.21 us -> 9.89 us
    dot_general x4 -> x0, matrix products: 3.5 us -> none  [the longest x3 2.44 us: matmul(): return jnp.dot(a, b, preferred_element_type=F32)]
    pallas_call x4 -> x2, Pallas kernels: 158 us -> 155 us  [the longest x1 102 us: margin_step(): pl.pallas_call(margin_kernel, in_specs=[anywhere] + [vmem] * 6, out_specs...]
  transfers between devices with their start and end apart: 2 -> 0, of which waited for: 1 -> 0; matrix products, arithmetic and copies ran while one was open for 5% -> 0% of each run, Pallas kernels for 35% -> 0%
where the time goes in v3:
time: 180 us
  Pallas kernels  155 us (86%)
  other arithmetic  12.6 us (7%)
  local copies, waits for them, and re-layouts  11.6 us (6%)
    pallas_call x1, Pallas kernels, margin_step(): pl.pallas_call(margin_kernel, in_specs=[anywhere] + [vmem] * 6, out_specs...  102 us
    pallas_call x1, Pallas kernels, fetch(): pl.pallas_call(fetch_kernel, in_specs=[vmem] * 4 + [anywhere], out_specs=...  53 us
    convert_element_type x1, other arithmetic, body(): centres_new = (centre_float - learn_rate * momentum_new).astype(BF16)  12.6 us
    unnamed x21, local copies, waits for them, and re-layouts  9.89 us

profile of v3, /device:TPU:0, one launch (start us, length us, event | category | flops | bytes accessed | tf_op | source)
XLA Modules:
  0.0 179.8 jit_solution(5084033811958493965)
XLA Ops:
  0.6 0.0 copy-start
  0.7 2.2 %copy-done = bf16[4096,512]{1,0:T(8,128)(2,1)S(1)} copy-done((bf16[4096,512]{1,0:T(8,128)(2,1)S(1)}, bf16[4096,512]{1,0:T(8,128)(2,1)}, u32[]{:S(2)}) %copy-start) | copy-done | bytes 4194328
  2.8 0.0 copy-start.3
  2.8 0.8 copy-done.3
  3.7 0.0 copy-start.5
  3.7 0.7 copy-done.5
  4.4 0.0 copy-start.6
  4.4 0.7 copy-done.6
  5.1 0.0 copy-start.7
  5.1 0.7 copy-done.7
  5.8 53.0 %fetch.1 = (bf16[4,4,4,64,512]{4,3,2,1,0:T(8,128)(2,1)S(1)}, bf16[512,512]{1,0:T(8,128)(2,1)S(1)}, s32[512,1]{1,0:T(8,128)S(1)}, s32[1,512]{1,0:T(1,128)S(1)}, s...) custom-call(bf16[64,512]{1,0:T(8,128)(2,1)S(1)} %copy-done.3, s32[1,2048]{1,0:T(1,128)S(1)} %bitcast.13, ...), custom_call_target="tpu_custom_call" | custom-call | tf_op jit(solution)/shard_map/fetch/pallas_call | solution.py:270
  58.8 0.0 copy-start.1
  58.8 2.0 %copy-done.1 = bf16[4,4,4,64,512]{4,3,2,1,0:T(8,128)(2,1)} copy-done((bf16[4,4,4,64,512]{4,3,2,1,0:T(8,128)(2,1)}, bf16[4,4,4,64,512]{4,3,2,1,0:T(8,128)(2,1)S(1)}, u32[]{:S(2)}) %copy-start.1) | copy-done | bytes 4194328
  60.8 0.0 copy-start.2
  60.8 0.8 copy-done.2
  61.6 0.0 copy-start.4
  61.6 0.7 copy-done.4
  62.3 0.0 copy-start.8
  62.3 0.6 copy-done.8
  62.9 0.1 sub.17
  63.1 0.7 sub.19.labels_ref
  63.8 0.2 slice_reduce_fusion
  63.9 0.7 reshape_squeeze.3.index_ref
  64.6 101.9 %margin_step.1 = (f32[8,512,512]{2,1,0:T(8,128)}, f32[64,512]{1,0:T(8,128)}) custom-call(bf16[4,16,64,512]{3,2,1,0:T(8,128)(2,1)} %bitcast.12, bf16[512,512]{1,0:T(8,128)(2,1)} %copy-done.2, s32[16,512]{1,0:T(8,128)} %sub.19.labels_ref, s32[512,1]{1,0:T(8,128)} %copy-done.4, s32[1,512]{1,0:T(1,128)} %copy-done.8, s32[4,1,1024]{2,1,0:T(1,128)} %reshape_squeeze.3.index_ref, ...), custom_call_target="tpu_custom_call" | custom-call | tf_op jit(solution)/shard_map/margin_step/pallas_call | solution.py:621
  166.5 0.0 copy-start.9
  166.5 12.6 %fusion.1 = (bf16[4096,512]{1,0:T(8,128)(2,1)}, f32[4096,512]{1,0:T(8,128)}) fusion(bf16[4096,512]{1,0:T(8,128)(2,1)} %centres_hbm.1, f32[8,512,512]{2,1,0:T(8,128)} %get-tuple-element.18, f32[4096,512]{1,0:T(8,128)} %param.9), kind=kLoop, calls=%fused_computation.3 | loop fusion | flops 16777216 | bytes 33554432 | tf_op jit(solution)/shard_map/convert_element_type | solution.py:691
  179.2 0.0 copy-done.9
  179.2 0.7 copy.13
  (2 shorter events, 0.1 us)
Async XLA Ops:
  0.6 2.2 %copy-start = (bf16[4096,512]{1,0:T(8,128)(2,1)S(1)}, bf16[4096,512]{1,0:T(8,128)(2,1)}, u32[]{:S(2)}) copy-start(bf16[4096,512]{1,0:T(8,128)(2,1)} %centres_hbm.1) | copy-start | bytes 12582916
  2.8 0.8 copy-start.3
  3.7 0.7 copy-start.5
  4.4 0.7 copy-start.6
  5.1 0.7 copy-start.7
  58.8 2.0 %copy-start.1 = (bf16[4,4,4,64,512]{4,3,2,1,0:T(8,128)(2,1)}, bf16[4,4,4,64,512]{4,3,2,1,0:T(8,128)(2,1)S(1)}, u32[]{:S(2)}) copy-start(bf16[4,4,4,64,512]{4,3,2,1,0:T(8,128)(2,1)S(1)} %get-tuple-element.11) | copy-start | bytes 12582916
  60.8 0.8 copy-start.2
  61.6 0.8 copy-start.4
  62.3 0.6 copy-start.8
  166.5 12.6 %copy-start.9 = (f32[64,512]{1,0:T(8,128)S(1)}, f32[64,512]{1,0:T(8,128)}, u32[]{:S(2)}) copy-start(f32[64,512]{1,0:T(8,128)} %get-tuple-element.24) | copy-start | bytes 393220

commit v4 on v3

v4 whole, which is shorter than its diff:
```python
import jax
import jax.numpy as jnp
from jax import lax
from jax.experimental import pallas as pl
from jax.experimental.pallas import tpu as pltpu
from jax.sharding import Mesh
from jax.sharding import PartitionSpec as P

CLS = ("cls_0", "cls_1", "cls_2")
DP_CLS = ("dp", "cls_0", "cls_1", "cls_2")

eps = 1e-06
logit_scale = 64.0
margin = 0.35
momentum_rate = 0.9
learn_rate = 0.1
weight_decay = 0.0005
BF16 = jnp.bfloat16
F32 = jnp.float32


MESH = pl.DeviceIdType.MESH
N_TILES = 32
ACROSS = 4


def where_am_i():
    z, y, x, c = (lax.axis_index(name) for name in DP_CLS)
    return z, y, x, c, y * 8 + x * 2 + c


def ahead(position, k):
    return lax.rem(position + k, ACROSS)


def tile_device(z, t):
    return (z, lax.div(t, 8), lax.rem(lax.div(t, 2), ACROSS), lax.rem(t, 2))


def remote(src, dst, send, recv, device):
    return pltpu.make_async_remote_copy(
        src_ref=src, dst_ref=dst, send_sem=send, recv_sem=recv, device_id=device, device_id_type=MESH
    )


def greet(devices, tiles=None):
    barrier = pltpu.get_barrier_semaphore()
    for device in devices:
        pl.semaphore_signal(barrier, inc=1, device_id=device, device_id_type=MESH)
    count = len(devices)
    if tiles is not None:
        z, me = tiles

        @pl.loop(1, N_TILES)
        def _(k):
            pl.semaphore_signal(
                barrier, inc=1, device_id=tile_device(z, lax.rem(me + k, N_TILES)), device_id_type=MESH
            )

        count += N_TILES - 1
    return barrier, count


def by_lanes(a, b):
    return lax.dot_general(a, b, (((1,), (1,)), ((), ())), preferred_element_type=F32)


def flag(condition):
    return jnp.where(condition, 1.0, 0.0)


def iota(shape, dim):
    return lax.broadcasted_iota(jnp.int32, shape, dim)


def plan_request(home, row, group):
    columns = home.shape[1]
    block = 128
    cuts = [slice(b * block, (b + 1) * block) for b in range(columns // block)]
    at_home = flag(iota((N_TILES, columns), 0) == home)
    upper = flag(iota((block, block), 0) < iota((block, block), 1)).astype(BF16)
    stacked = jnp.concatenate([at_home[:, cut] for cut in cuts], axis=0).astype(BF16)
    within = jnp.dot(stacked, upper, preferred_element_type=F32)
    before = [jnp.zeros((N_TILES, 1), F32)]
    for cut in cuts:
        before.append(before[-1] + jnp.sum(at_home[:, cut], axis=1, keepdims=True))
    count = jnp.broadcast_to(before[-1], (N_TILES, block)).astype(BF16)
    lower = flag(iota((N_TILES, N_TILES), 1) < iota((N_TILES, N_TILES), 0)).astype(BF16)
    offset = jnp.dot(lower, count, preferred_element_type=F32)
    first = ((offset.astype(jnp.int32) + (ACROSS - 1 - group)) >> 2).astype(F32)
    places, starts = [], []
    for b, cut in enumerate(cuts):
        mark = at_home[:, cut]
        rank = within[b * N_TILES : (b + 1) * N_TILES] + before[b] + offset
        places.append(jnp.sum(mark * rank, axis=0, keepdims=True))
        starts.append(jnp.sum(mark * first, axis=0, keepdims=True))
    place = jnp.concatenate(places, axis=1).astype(jnp.int32)
    start = jnp.concatenate(starts, axis=1).astype(jnp.int32)
    mine = (place & 3) == group
    kept = place >> 2
    slot = kept - start
    by_slot = flag(mine & (iota((block, columns), 0) == slot)).astype(BF16)
    digits = [at_home * (row >> 6).astype(F32), at_home * (row & 63).astype(F32)]
    asked = by_lanes(jnp.concatenate(digits, axis=0).astype(BF16), by_slot)
    return (asked[:N_TILES] * 64 + asked[N_TILES:]).astype(jnp.int32), mine, kept, slot


def plan_kept(home, mine, kept, slot, slots):
    columns, block = home.shape[1], 128
    by_kept = flag(mine & (iota((block, columns), 0) == (kept & 127))).astype(BF16)
    lane = iota((1, columns), 1)
    parts = []
    for value in (home, slot, lane >> 6, lane & 63):
        for a in range(ACROSS):
            parts.append(jnp.where((kept >> 7) == a, value.astype(F32), 0.0))
    found = by_lanes(jnp.concatenate(parts, axis=0).astype(BF16), by_kept)
    turned = jnp.concatenate([found, jnp.zeros((block - found.shape[0], block), F32)], axis=0).T
    runs = range(ACROSS)
    slot_row = jnp.concatenate([found[a : a + 1] * slots + found[4 + a : 5 + a] for a in runs], axis=1)
    slot_column = jnp.concatenate([turned[:, a : a + 1] * slots + turned[:, 4 + a : 5 + a] for a in runs], axis=0)
    column = jnp.concatenate([turned[:, 8 + a : 9 + a] * 64 + turned[:, 12 + a : 13 + a] for a in runs], axis=0)
    return slot_row.astype(jnp.int32), slot_column.astype(jnp.int32), column.astype(jnp.int32)


def step_kernel(
    emb_hbm, home_hbm, row_hbm, labels_hbm, centres_hbm, momentum_hbm, momentum_out, emb_out,
    emb, home, row, labels_here, labels_all, labels_at, labels, request, incoming, index_all, index,
    column, slot_row, xall, expo, den, got, inverse, acc, fetched, wunit, scaled, turned, replies, replied, packed, arrived,
    nearby, over, came, mine, first_a, first_b, next_a, next_b, second_a, second_b, last, third,
    local_sem, request_sent, request_came, reply_sent, reply_came, tell_sent, tell_came, phase_sent, phase_came,
    x_sent, x_came, den_sent, den_came, row_sent, row_came, ring_sent, ring_came, over_sent, over_came,
    step_sent, step_came,
):
    z, y, x, c, me = where_am_i()
    other = 1 - c
    partner = (z, y, x, other)
    others = range(ACROSS - 1)
    along_x = [(z, y, ahead(x, k + 1), c) for k in others]
    along_y = [(z, ahead(y, k + 1), x, c) for k in others]
    along_z = [(ahead(z, k + 1), y, x, c) for k in others]
    along = {"x": along_x, "y": along_y, "z": along_z}
    pieces = 8
    slots = packed.shape[1]
    block, width = expo.shape[1], expo.shape[2]
    kept = block
    lanes = width // 2

    def local(src, dst, n):
        return pltpu.make_async_copy(src, dst, local_sem.at[n])

    def load_centres(i):
        rows, columns = pl.ds(block * (i // 2), block), pl.ds(lanes * (i % 2), lanes)
        return local(centres_hbm.at[rows, columns], over.at[i], 8 + i)

    small = [
        local(src, dst, n)
        for n, (src, dst) in enumerate(
            ((home_hbm, home), (row_hbm, row), (emb_hbm, emb), (labels_hbm, labels_here))
        )
    ]
    for copy in small:
        copy.start()
    for i in range(2 * pieces):
        load_centres(i).start()
    barrier, count = greet(along_z, (z, me))
    for copy in small:
        copy.wait()
    xfloat = emb[...].astype(F32)
    row_norm = jnp.sqrt(jnp.sum(xfloat * xfloat, axis=1, keepdims=True) + eps)
    xall[c, z, y, x] = (xfloat / row_norm).astype(BF16)

    def ask(k):
        t = lax.rem(me + k, N_TILES)
        return remote(request.at[t], incoming.at[me], request_sent.at[t], request_came.at[me], tile_device(z, t))

    def asked_by(t):
        return remote(request.at[t], incoming.at[t], request_sent.at[t], request_came.at[t], tile_device(z, t))

    def answer(t):
        return remote(replies.at[t], replied.at[me], reply_sent.at[t], reply_came.at[me], tile_device(z, t))

    def answered(t):
        return remote(replies.at[t], replied.at[t], reply_sent.at[t], reply_came.at[t], tile_device(z, t))

    parts = ((0, 16, "zxy"), (16, 16, "zyx"), (32, 32, "xyz"))
    place = {"z": z, "y": y, "x": x}

    def held(part, phase, position, cut=None):
        first, size, axes = parts[part]
        at = dict(place)
        for n in range(phase):
            at[axes[n]] = pl.ds(0, ACROSS)
        if cut is not None:
            at[axes[0]] = pl.ds(2 * cut, 2)
        at[axes[phase]] = position
        return xall.at[c, at["z"], at["y"], at["x"], pl.ds(first, size)]

    def spread(part, phase, kind):
        axis = parts[part][2][phase]
        position, peers = place[axis], along[axis]
        n = 4 * (3 * part + phase)

        def one(k, ref, peer):
            return remote(ref, ref, phase_sent.at[n + k], phase_came.at[n + k], peers[peer])

        if phase == 0:
            mine_here = held(part, phase, position)
            return [one(k, mine_here, k) for k in others] if kind == 0 else []
        if kind == 0:
            mine_here = held(part, phase, position)
            return [one(0, mine_here, 0), one(1, mine_here, 2)]
        return [
            one(2, held(part, phase, ahead(position, 3), 0), 0),
            one(3, held(part, phase, ahead(position, 1), 1), 2),
        ]

    flying = []

    def send(copies):
        for copy in copies:
            copy.start()
        flying.extend(copies)

    def land(copies):
        for copy in copies:
            copy.wait_recv()

    tell = [
        remote(labels_here, labels_all.at[k], tell_sent.at[k], tell_came.at[k], along_z[k]) for k in others
    ]
    pl.semaphore_wait(barrier, count)
    for part in (2, 0, 1):
        send(spread(part, 0, 0))
    asked, taken, kept_as, slot_at = plan_request(home[...], row[...], z)
    request[...] = asked.reshape(request.shape)

    @pl.loop(1, N_TILES)
    def _(k):
        ask(k).start()

    send(tell)
    incoming[me] = request[me]
    for part in (2, 0, 1):
        land(spread(part, 0, 0))
        send(spread(part, 1, 0))
    slot_row[...], slot_column, column[...] = plan_kept(home[...], taken, kept_as, slot_at, slots)
    for part in (2, 0, 1):
        land(spread(part, 1, 0))
        send(spread(part, 1, 1))

    @pl.loop(1, N_TILES)
    def _(k):
        asked_by(lax.rem(me + k, N_TILES)).wait_recv()

    share = [
        remote(incoming, index_all.at[k], tell_sent.at[3 + k], tell_came.at[3 + k], along_z[k]) for k in others
    ]
    send(share)
    for i in range(2 * pieces):
        load_centres(i).wait()
    row_ids = iota((slots, pieces * block), 1)
    for turn, q in enumerate((1, 2, 3, 0)):
        first = ahead(y, q) * 8
        wanted = incoming[pl.ds(first, 8)].reshape(8, 128).T
        pick = jnp.concatenate(
            [flag(row_ids == wanted[:slots, j : j + 1]).astype(BF16) for j in range(8)], axis=0
        )
        found = []
        for h in range(2):
            half_found = jnp.zeros((8 * slots, lanes), F32)
            for r in range(pieces):
                half_found += jnp.dot(
                    pick[:, r * block : (r + 1) * block], over[2 * r + h], preferred_element_type=F32
                )
            found.append(half_found.astype(BF16))
        replies[pl.ds(first, 8)] = jnp.concatenate(found, axis=1).reshape(8, slots, width)
        for j in range(8):
            if q:
                answer(first + j).start()
            else:

                @pl.when(first + j != me)
                def _(t=first + j):
                    answer(t).start()

        if turn == 0:
            for part in (2, 0, 1):
                land(spread(part, 1, 1))
                send(spread(part, 2, 0))

    replied[me] = replies[me]
    land(tell + share)
    labels_at[z] = labels_here[...]
    for k in others:
        labels_at[ahead(z, 3 - k)] = labels_all[k]
    rows = emb.shape[0]
    for side in range(2):
        for i in range(pieces):
            runs = [
                labels_at[g, 2 * i + j : 2 * i + j + 1, side * rows : (side + 1) * rows]
                for j in range(2)
                for g in range(ACROSS)
            ]
            labels[side * pieces + i : side * pieces + i + 1] = (
                jnp.concatenate(runs, axis=1) - me * home.shape[1]
            )

    def along_lanes(ref):
        return jnp.concatenate([ref[t][:, :slots] for t in range(N_TILES)], axis=1)

    index[0] = along_lanes(incoming)
    for n, k in ((1, 2), (2, 0), (3, 1)):
        index[n] = along_lanes(index_all.at[k])
    for part in (0, 1, 2):
        land(spread(part, 2, 0))
        send(spread(part, 2, 1))

    @pl.loop(1, N_TILES)
    def _(k):
        answered(lax.rem(me + k, N_TILES)).wait_recv()

    pick = flag(slot_column == iota((kept, N_TILES * slots), 1)).astype(BF16)
    wfloat = jnp.dot(pick, replied[...].reshape(N_TILES * slots, width), preferred_element_type=F32)
    fetched[...] = wfloat.astype(BF16)
    col_norm = jnp.sqrt(jnp.sum(wfloat * wfloat, axis=1, keepdims=True) + eps)
    wunit[...] = wfloat / col_norm
    scaled[...] = (logit_scale * wunit[...]).astype(BF16)
    turned[...] = wunit[...].T.astype(BF16)

    def swap_part(part, slot):
        first, size, _ = parts[part]
        ref = xall.at[slot, :, :, :, pl.ds(first, size)]
        return remote(ref, ref, x_sent.at[pieces + part], x_came.at[pieces + part], partner)

    def swap_piece(i, slot):
        first, size, _ = parts[2]
        ref = xall.at[slot, :, lax.div(i, 2), pl.ds(2 * lax.rem(i, 2), 2), pl.ds(first, size)]
        return remote(ref, ref, x_sent.at[i], x_came.at[i], partner)

    for part in (0, 1):
        land(spread(part, 2, 1))
        swap_part(part, c).start()
    land(spread(2, 2, 1))

    @pl.loop(0, pieces)
    def _(i):
        swap_piece(i, c).start()

    for part in (0, 1):
        swap_part(part, other).wait_recv()

    def rows_of(side, i):
        y_of, x_of = lax.div(i, 2), 2 * lax.rem(i, 2)
        return jnp.concatenate(
            [xall[side, g, y_of, x_of + j] for j in range(2) for g in range(ACROSS)], axis=0
        )

    def exponents(group, i):
        swap_piece(i, other).wait_recv()
        for side in range(2):
            logit = by_lanes(scaled[...], rows_of(side, i))
            hit = column[...] == labels[pl.ds(side * pieces + i, 1)]
            value = jnp.exp(jnp.where(hit, logit - logit_scale * margin, logit))
            expo[side * pieces + i] = value
            den[group, 0, pl.ds(2 * (i - 4 * group) + side, 1)] = jnp.sum(value, axis=0, keepdims=True)

    stages = ((0, [partner]), (1, along_x), (4, along_y), (7, along_z))

    def stage_copies(group, stage):
        slot, peers = stages[stage]
        return [
            remote(
                den.at[group, stage],
                got.at[group, slot + k],
                den_sent.at[10 * group + slot + k],
                den_came.at[10 * group + slot + k],
                peer,
            )
            for k, peer in enumerate(peers)
        ]

    def stage_start(group, stage):
        for copy in stage_copies(group, stage):
            copy.start()

    def stage_end(group, stage):
        for copy in stage_copies(group, stage):
            copy.wait()
        slot, peers = stages[stage]
        total = den[group, stage]
        for k in range(len(peers)):
            total = total + got[group, slot + k]
        if stage < 3:
            den[group, stage + 1] = total
            stage_start(group, stage + 1)
        else:
            inverse[group] = logit_scale / total

    def gradients(group, i):
        for side in range(2):
            b = side * pieces + i
            hit = column[...] == labels[pl.ds(b, 1)]
            share = expo[b] * inverse[group, pl.ds(2 * (i - 4 * group) + side, 1)]
            grad = jnp.where(hit, share - logit_scale, share).astype(BF16)
            expo[b] = grad.astype(F32)
            acc[...] += jnp.dot(grad, rows_of(side, i), preferred_element_type=F32)

    half = mine.shape[2] // 2
    low, high = pl.ds(0, half), pl.ds(half, half)

    def product(side, i):
        return jnp.dot(turned[...], expo[side * pieces + i].astype(BF16), preferred_element_type=F32)

    def hand_over(i):
        two = pl.ds(2 * i, 2)
        return remote(over.at[two], came.at[two], over_sent.at[i], over_came.at[i], partner)

    def give_over(i):
        part = product(other, i).astype(BF16)
        over[2 * i] = part[:, :lanes]
        over[2 * i + 1] = part[:, lanes:]
        hand_over(i).start()

    def own_part(i):
        part = product(c, i)
        hand_over(i).wait_recv()
        y_of, x_of = lax.div(i, 2), 2 * lax.rem(i, 2)
        mine[y_of, x_of] = (part[:, :lanes] + came[2 * i].astype(F32)).astype(BF16)
        mine[y_of, x_of + 1] = (part[:, lanes:] + came[2 * i + 1].astype(F32)).astype(BF16)

    acc[...] = jnp.zeros_like(acc)

    @pl.loop(0, 4)
    def _(i):
        exponents(0, i)

    stage_start(0, 0)
    for n in range(4):
        exponents(1, 4 + n)
        if n == 3:
            stage_start(1, 0)
        stage_end(0, n)
    for n in range(4):
        gradients(0, n)
        give_over(n)
        if n:
            own_part(n - 1)
        stage_end(1, n)
    own_part(3)

    @pl.loop(4, pieces)
    def _(i):
        gradients(1, i)

    dwhat = acc[...]
    unit = wunit[...]
    wfloat = fetched[...].astype(F32)
    col_norm = jnp.sqrt(jnp.sum(wfloat * wfloat, axis=1, keepdims=True) + eps)
    dfetched = ((dwhat - unit * jnp.sum(unit * dwhat, axis=1, keepdims=True)) / col_norm).astype(BF16)
    pick = flag(slot_row[...] == iota((N_TILES * slots, kept), 0)).astype(BF16)
    packed[...] = jnp.dot(pick, dfetched, preferred_element_type=F32).astype(BF16).reshape(packed.shape)

    def give(t):
        return remote(packed.at[t], arrived.at[me], row_sent.at[t], row_came.at[me], tile_device(z, t))

    def given(t):
        return remote(packed.at[t], arrived.at[t], row_sent.at[t], row_came.at[t], tile_device(z, t))

    for q in range(ACROSS):
        for j in range(8):
            if q:
                give(8 * ahead(y, q) + j).start()
            else:

                @pl.when(8 * y + j != me)
                def _(t=8 * y + j):
                    give(t).start()

    arrived[me] = packed[me]

    def tiles_of(n):
        return pl.ds(8 * ahead(y, (ACROSS - n) % ACROSS), 8)

    def down(n):
        return remote(
            arrived.at[tiles_of(n)], nearby.at[0, tiles_of(n)], ring_sent.at[n], ring_came.at[n], along_z[2]
        )

    def up(n):
        return remote(
            arrived.at[tiles_of(n)], nearby.at[1, tiles_of(n)], ring_sent.at[4 + n], ring_came.at[4 + n], along_z[0]
        )

    def onward(n):
        source, device = (1, along_z[0]) if n < 2 else (0, along_z[2])
        return remote(
            nearby.at[source, tiles_of(n)],
            nearby.at[2, tiles_of(n)],
            ring_sent.at[8 + n],
            ring_came.at[8 + n],
            device,
        )

    def pass_on(n):
        for j in range(8):
            t = 8 * ahead(y, (ACROSS - n) % ACROSS) + j
            if n:
                given(t).wait_recv()
            else:

                @pl.when(t != me)
                def _(t=t):
                    given(t).wait_recv()

        up(n).start()
        down(n).start()

    pl.loop(4, 8)(give_over)
    pass_on(0)
    pl.loop(4, 8)(own_part)
    pass_on(1)

    def sum_over(n, position, peers, part, inbox):
        up_at, far_at, down_at = (ahead(position, k) for k in (1, 2, 3))

        def hop(k, src, dst, device):
            return remote(src, dst, step_sent.at[n + k], step_came.at[n + k], device)

        early = [
            hop(0, part(far_at, 0), inbox.at[2, 0], peers[0]),
            hop(1, part(far_at, 1), inbox.at[2, 1], peers[2]),
            hop(2, part(up_at, 1), inbox.at[0, 1], peers[0]),
            hop(3, part(down_at, 0), inbox.at[1, 0], peers[2]),
        ]
        late = [hop(4, part(up_at, 0), inbox.at[0, 0], peers[0]), hop(5, part(down_at, 1), inbox.at[1, 1], peers[2])]
        for copy in early:
            copy.start()

        def relay():
            for k, ref in ((0, part(up_at, 0)), (1, part(down_at, 1))):
                early[k].wait_recv()
                ref[...] = (ref[...].astype(F32) + inbox[2, k].astype(F32)).astype(BF16)
                late[k].start()
            flying.extend(early + late)

        return relay, early[2:] + late

    relay_a, rest_a = sum_over(0, x, along_x, lambda p, h: mine.at[pl.ds(2 * h, 2), p, low], first_a)
    relay_b, rest_b = sum_over(6, y, along_y, lambda p, h: mine.at[p, pl.ds(2 * h, 2), high], first_b)

    pass_on(2)
    pass_on(3)

    @pl.loop(0, pieces)
    def _(i):
        hand_over(i).wait_send()

    old = local(momentum_hbm, expo.at[pl.ds(pieces, pieces)], 4)
    old.start()
    for i in range(2 * pieces):
        load_centres(i).start()
    old.wait()
    for i in range(2 * pieces):
        load_centres(i).wait()

    def save(r):
        return local(expo.at[r], momentum_out.at[r], 8 + r)

    def scatter(n, rows_ref, fresh=False, final=False):
        slot_rows = rows_ref.reshape(N_TILES * slots, width)
        wanted = index[n]

        @pl.loop(0, pieces)
        def _(r):
            pick = flag(iota((block, N_TILES * slots), 0) + r * block == wanted).astype(BF16)
            grad = jnp.dot(pick, slot_rows, preferred_element_type=F32)
            if fresh:
                centre = jnp.concatenate([over[2 * r], over[2 * r + 1]], axis=1).astype(F32)
                grad = momentum_rate * expo[pieces + r] + grad + weight_decay * centre
                expo[r] = grad
            else:
                expo[r] = expo[r] + grad
            if final:
                save(r).start()

    for n in range(2):
        up(n).wait_recv()
        onward(n).start()
    scatter(0, arrived[...], fresh=True)
    relay_a()
    relay_b()
    down(2).wait_recv()
    onward(2).start()
    land(rest_a + rest_b)

    @pl.loop(0, ACROSS)
    def _(i):
        h, j = lax.div(i, 2), lax.rem(i, 2)
        total, below = mine[i, x, low].astype(F32), mine[y, i, high].astype(F32)
        for k in range(2):
            total = total + first_a[k, h, j].astype(F32)
            below = below + first_b[k, h, j].astype(F32)
        next_a[i] = total.astype(BF16)
        next_b[i] = below.astype(BF16)

    quarter = half // 2
    relay_a, rest_a = sum_over(12, y, along_y, lambda p, h: next_a.at[p, pl.ds(quarter * h, quarter)], second_a)
    relay_b, rest_b = sum_over(18, x, along_x, lambda p, h: next_b.at[p, pl.ds(quarter * h, quarter)], second_b)
    down(3).wait_recv()
    onward(3).start()
    relay_a()
    relay_b()
    for n in range(2):
        down(n).wait_recv()
    scatter(1, nearby[0])
    for n in range(2, 4):
        up(n).wait_recv()
    scatter(2, nearby[1])
    land(rest_a + rest_b)
    top, bottom = next_a[y].astype(F32), next_b[x].astype(F32)
    for k in range(2):
        top = top + second_a[k].astype(F32).reshape(half, lanes)
        bottom = bottom + second_b[k].astype(F32).reshape(half, lanes)
    last[:, :, :half] = top.T.astype(BF16).reshape(ACROSS, rows, half)
    last[:, :, half:] = bottom.T.astype(BF16).reshape(ACROSS, rows, half)
    three = [
        remote(last.at[ahead(z, k + 1)], third.at[k], step_sent.at[24 + k], step_came.at[24 + k], along_z[k])
        for k in others
    ]
    send(three)
    land([onward(n) for n in range(4)])
    scatter(3, nearby[2], final=True)
    xfloat = emb[...].astype(F32)
    row_norm = jnp.sqrt(jnp.sum(xfloat * xfloat, axis=1, keepdims=True) + eps)
    xunit = xfloat / row_norm
    land(three)
    dunit = last[z].astype(F32)
    for k in others:
        dunit = dunit + third[k].astype(F32)
    emb_out[...] = (dunit - xunit * jnp.sum(xunit * dunit, axis=1, keepdims=True)) / row_norm
    for copy in flying:
        copy.wait_send()
    for n in range(4):
        up(n).wait_send()
        down(n).wait_send()
        onward(n).wait_send()
    for part in (0, 1):
        swap_part(part, c).wait_send()

    @pl.loop(0, pieces)
    def _(i):
        swap_piece(i, c).wait_send()

    @pl.loop(1, N_TILES)
    def _(k):
        ask(k).wait_send()
        answer(lax.rem(me + k, N_TILES)).wait_send()
        give(lax.rem(me + k, N_TILES)).wait_send()

    @pl.loop(0, pieces)
    def _(r):
        save(r).wait()


def step(embeddings, home, row, labels, centres, momentum):
    rows, width = embeddings.shape
    columns = home.shape[1]
    homes = centres.shape[0]
    kept = columns // ACROSS
    slots = 2 * kept // N_TILES
    block, blocks = kept, 2 * rows * ACROSS**3 // kept
    half, lanes = width // 2, width // 2
    there, vmem = pl.BlockSpec(memory_space=pltpu.HBM), pl.BlockSpec(memory_space=pltpu.VMEM)
    small = [(16, 128), (ACROSS - 1, 16, 128), (ACROSS, 16, 128), (blocks, block), (N_TILES, 1, 128), (N_TILES, 1, 128)]
    small += [(ACROSS - 1, N_TILES, 1, 128), (ACROSS, 1, N_TILES * slots), (kept, 1), (1, kept)]
    sums = [(2, 4, blocks // 2, block), (2, 10, blocks // 2, block), (2, blocks // 2, block), (kept, width)]
    halves = [(blocks, width, lanes)] * 2 + [(ACROSS, ACROSS, width, lanes)] + [(3, 2, 2, half, lanes)] * 2
    halves += [(ACROSS, half, lanes)] * 2 + [(3, 2, half // 2, lanes)] * 2 + [(ACROSS, rows, width), (3, rows, width)]
    sems = [24, N_TILES, N_TILES, N_TILES, N_TILES, 6, 6, 36, 36, 10, 10, 20, 20, N_TILES, N_TILES, 12, 12, 8, 8, 27, 27]
    return pl.pallas_call(
        step_kernel,
        in_specs=[there] * 6,
        out_specs=[there, vmem],
        out_shape=[
            jax.ShapeDtypeStruct((homes // block, block, width), F32),
            jax.ShapeDtypeStruct((rows, width), F32),
        ],
        scratch_shapes=[
            pltpu.VMEM((rows, width), BF16),
            pltpu.VMEM((1, columns), jnp.int32),
            pltpu.VMEM((1, columns), jnp.int32),
        ]
        + [pltpu.VMEM(shape, jnp.int32) for shape in small]
        + [
            pltpu.VMEM((2, ACROSS, ACROSS, ACROSS, rows, width), BF16),
            pltpu.VMEM((blocks, kept, block), F32),
        ]
        + [pltpu.VMEM(shape, F32) for shape in sums]
        + [pltpu.VMEM((kept, width), BF16), pltpu.VMEM((kept, width), F32)]
        + [pltpu.VMEM((kept, width), BF16), pltpu.VMEM((width, kept), BF16)]
        + [pltpu.VMEM((N_TILES, slots, width), BF16)] * 4
        + [pltpu.VMEM((3, N_TILES, slots, width), BF16)]
        + [pltpu.VMEM(shape, BF16) for shape in halves]
        + [pltpu.SemaphoreType.DMA((n,)) for n in sems],
        compiler_params=pltpu.CompilerParams(
            collective_id=0, has_side_effects=True, vmem_limit_bytes=60 * 2**20
        ),
        name="step",
    )(embeddings, home, row, labels, centres, momentum.reshape(homes // block, block, width))


def finish_kernel(new_ref, centres_ref, emb_ref, momentum_out, centres_out, emb_out):
    momentum = new_ref[...]
    momentum_out[...] = momentum
    centres_out[...] = (centres_ref[...].astype(F32) - learn_rate * momentum).astype(BF16)
    emb_out[...] = emb_ref[...]


def finish(new, centres, emb_grad, rows=512):
    homes, width = centres.shape
    part = pl.BlockSpec((rows, width), lambda i: (i, 0))
    whole = pl.BlockSpec(emb_grad.shape, lambda i: (0, 0))
    return pl.pallas_call(
        finish_kernel,
        grid=(homes // rows,),
        in_specs=[part, part, whole],
        out_specs=[part, part, whole],
        out_shape=[
            jax.ShapeDtypeStruct((homes, width), F32),
            jax.ShapeDtypeStruct((homes, width), BF16),
            jax.ShapeDtypeStruct(emb_grad.shape, F32),
        ],
        compiler_params=pltpu.CompilerParams(vmem_limit_bytes=60 * 2**20),
        name="finish",
    )(new, centres, emb_grad)


def body(embeddings, labels, centres, momentum, sample_home, sample_row):
    columns = sample_row.shape[0]
    new, emb_grad = step(
        embeddings,
        sample_home.reshape(1, columns),
        sample_row.reshape(1, columns),
        labels.reshape(16, 128),
        centres,
        momentum,
    )
    momentum_new, centres_new, emb_grad = finish(new.reshape(centres.shape), centres, emb_grad)
    return (emb_grad, momentum_new, centres_new)


def solution(mesh):
    torus = Mesh(mesh.devices.reshape(mesh.shape["dp"], 4, 4, 2), ("dp", "cls_0", "cls_1", "cls_2"))
    return jax.shard_map(
        body,
        mesh=torus,
        in_specs=(P(DP_CLS, None), P("dp"), P(CLS, None), P(CLS, None), P(CLS, None), P(CLS)),
        out_specs=(P(DP_CLS, None), P(CLS, None), P(CLS, None)),
        check_vma=False,
    )
```

time: 180 us -> 157 us (0.87)
  other arithmetic: 12.6 us -> 0 us
  local copies, waits for them, and re-layouts: 11.6 us -> 0 us
    convert_element_type x1 -> x0, other arithmetic: 12.6 us -> none  [body(): centres_new = (centre_float - learn_rate * momentum_new).astype(BF16)]
    unnamed x21 -> x0, local copies, waits for them, and re-layouts: 9.89 us -> none
where the time goes in v4:
time: 157 us
  Pallas kernels  156 us (99%)
    pallas_call x1, Pallas kernels, step(): pl.pallas_call(step_kernel, in_specs=[there] * 6, out_specs=[there, vmem]...  145 us
    pallas_call x1, Pallas kernels, finish(): pl.pallas_call(finish_kernel, grid=(homes // rows,), in_specs=[part, part...  11.6 us

profile of v4, /device:TPU:0, one launch (start us, length us, event | category | flops | bytes accessed | tf_op | source)
XLA Modules:
  0.0 156.8 jit_solution(13802535637747560823)
XLA Ops:
  0.6 144.6 %step.1 = (f32[8,512,512]{2,1,0:T(8,128)}, f32[64,512]{1,0:T(8,128)}) custom-call(bf16[64,512]{1,0:T(8,128)(2,1)} %emb_hbm.1, s32[1,2048]{1,0:T(1,128)} %bitcast.7, s32[1,2048]{1,0:T(1,128)} %bitcast.8, s32[16,128]{1,0:T(8,128)} %bitcast.9, bf16[4096,512]{1,0:T(8,128)(2,1)} %centres_ref.1, f32[8,512,512]{2,1,0:T(8,128)} %bitcast.6), custom_call_target="tpu_custom_call" | custom-call | tf_op jit(solution)/shard_map/step/pallas_call | solution.py:680
  145.2 11.6 %finish.1 = (f32[4096,512]{1,0:T(8,128)}, bf16[4096,512]{1,0:T(8,128)(2,1)}, f32[64,512]{1,0:T(8,128)}) custom-call(f32[4096,512]{1,0:T(8,128)} %bitcast.5, bf16[4096,512]{1,0:T(8,128)(2,1)} %centres_ref.1, f32[64,512]{1,0:T(8,128)} %get-tuple-element.9.emb_ref), custom_call_target="tpu_custom_call" | custom-call | tf_op jit(solution)/shard_map/finish/pallas_call | solution.py:723

commit v5 on v4

--- a/solution.py
+++ b/solution.py
@@ -138,6 +138,7 @@
     along_x = [(z, y, ahead(x, k + 1), c) for k in others]
     along_y = [(z, ahead(y, k + 1), x, c) for k in others]
     along_z = [(ahead(z, k + 1), y, x, c) for k in others]
+    barrier, count = greet(along_z, (z, me))
     along = {"x": along_x, "y": along_y, "z": along_z}
     pieces = 8
     slots = packed.shape[1]
@@ -162,7 +163,6 @@
         copy.start()
     for i in range(2 * pieces):
         load_centres(i).start()
-    barrier, count = greet(along_z, (z, me))
     for copy in small:
         copy.wait()
     xfloat = emb[...].astype(F32)
@@ -198,20 +198,22 @@
     def spread(part, phase, kind):
         axis = parts[part][2][phase]
         position, peers = place[axis], along[axis]
-        n = 4 * (3 * part + phase)
+        n = 6 * (3 * part + phase)
 
         def one(k, ref, peer):
             return remote(ref, ref, phase_sent.at[n + k], phase_came.at[n + k], peers[peer])
 
         if phase == 0:
-            mine_here = held(part, phase, position)
-            return [one(k, mine_here, k) for k in others] if kind == 0 else []
+            whole = held(part, phase, position)
+            return [one(k, whole, k) for k in others]
+        here = [held(part, phase, position, cut) for cut in range(2)]
         if kind == 0:
-            mine_here = held(part, phase, position)
-            return [one(0, mine_here, 0), one(1, mine_here, 2)]
+            return [one(0, here[0], 0), one(1, here[1], 2)]
+        if kind == 1:
+            return [one(2, here[1], 0), one(3, here[0], 2)]
         return [
-            one(2, held(part, phase, ahead(position, 3), 0), 0),
-            one(3, held(part, phase, ahead(position, 1), 1), 2),
+            one(4, held(part, phase, ahead(position, 3), 0), 0),
+            one(5, held(part, phase, ahead(position, 1), 1), 2),
         ]
 
     flying = []
@@ -224,6 +226,18 @@
     def land(copies):
         for copy in copies:
             copy.wait_recv()
+
+    def begin(part, phase):
+        send(spread(part, phase, 0))
+        send(spread(part, phase, 1))
+
+    def forward(part, phase):
+        land(spread(part, phase, 0))
+        send(spread(part, phase, 2))
+
+    def end(part, phase):
+        land(spread(part, phase, 1))
+        land(spread(part, phase, 2))
 
     tell = [
         remote(labels_here, labels_all.at[k], tell_sent.at[k], tell_came.at[k], along_z[k]) for k in others
@@ -233,6 +247,9 @@
         send(spread(part, 0, 0))
     asked, taken, kept_as, slot_at = plan_request(home[...], row[...], z)
     request[...] = asked.reshape(request.shape)
+    for part in (2, 0, 1):
+        land(spread(part, 0, 0))
+        begin(part, 1)
 
     @pl.loop(1, N_TILES)
     def _(k):
@@ -240,13 +257,12 @@
 
     send(tell)
     incoming[me] = request[me]
-    for part in (2, 0, 1):
-        land(spread(part, 0, 0))
-        send(spread(part, 1, 0))
     slot_row[...], slot_column, column[...] = plan_kept(home[...], taken, kept_as, slot_at, slots)
     for part in (2, 0, 1):
-        land(spread(part, 1, 0))
-        send(spread(part, 1, 1))
+        forward(part, 1)
+    for part in (2, 0, 1):
+        end(part, 1)
+        begin(part, 2)
 
     @pl.loop(1, N_TILES)
     def _(k):
@@ -283,10 +299,11 @@
                 def _(t=first + j):
                     answer(t).start()
 
-        if turn == 0:
-            for part in (2, 0, 1):
-                land(spread(part, 1, 1))
-                send(spread(part, 2, 0))
+        if turn == 2:
+            for part in (0, 1):
+                forward(part, 2)
+        if turn == 3:
+            forward(2, 2)
 
     replied[me] = replies[me]
     land(tell + share)
@@ -311,9 +328,6 @@
     index[0] = along_lanes(incoming)
     for n, k in ((1, 2), (2, 0), (3, 1)):
         index[n] = along_lanes(index_all.at[k])
-    for part in (0, 1, 2):
-        land(spread(part, 2, 0))
-        send(spread(part, 2, 1))
 
     @pl.loop(1, N_TILES)
     def _(k):
@@ -338,9 +352,9 @@
         return remote(ref, ref, x_sent.at[i], x_came.at[i], partner)
 
     for part in (0, 1):
-        land(spread(part, 2, 1))
+        end(part, 2)
         swap_part(part, c).start()
-    land(spread(2, 2, 1))
+    end(2, 2)
 
     @pl.loop(0, pieces)
     def _(i):
@@ -435,19 +449,23 @@
         exponents(0, i)
 
     stage_start(0, 0)
-    for n in range(4):
-        exponents(1, 4 + n)
-        if n == 3:
-            stage_start(1, 0)
+
+    @pl.loop(4, pieces)
+    def _(i):
+        exponents(1, i)
+
+    stage_start(1, 0)
+    for n in range(3):
         stage_end(0, n)
-    for n in range(4):
-        gradients(0, n)
-        give_over(n)
-        if n:
-            own_part(n - 1)
         stage_end(1, n)
-    own_part(3)
-
+    stage_end(0, 3)
+
+    @pl.loop(0, 4)
+    def _(i):
+        gradients(0, i)
+        give_over(i)
+
+    stage_end(1, 3)
     @pl.loop(4, pieces)
     def _(i):
         gradients(1, i)
@@ -517,7 +535,7 @@
 
     pl.loop(4, 8)(give_over)
     pass_on(0)
-    pl.loop(4, 8)(own_part)
+    pl.loop(0, 8)(own_part)
     pass_on(1)
 
     def sum_over(n, position, peers, part, inbox):
@@ -676,7 +694,7 @@
     sums = [(2, 4, blocks // 2, block), (2, 10, blocks // 2, block), (2, blocks // 2, block), (kept, width)]
     halves = [(blocks, width, lanes)] * 2 + [(ACROSS, ACROSS, width, lanes)] + [(3, 2, 2, half, lanes)] * 2
     halves += [(ACROSS, half, lanes)] * 2 + [(3, 2, half // 2, lanes)] * 2 + [(ACROSS, rows, width), (3, rows, width)]
-    sems = [24, N_TILES, N_TILES, N_TILES, N_TILES, 6, 6, 36, 36, 10, 10, 20, 20, N_TILES, N_TILES, 12, 12, 8, 8, 27, 27]
+    sems = [24, N_TILES, N_TILES, N_TILES, N_TILES, 6, 6, 54, 54, 10, 10, 20, 20, N_TILES, N_TILES, 12, 12, 8, 8, 27, 27]
     return pl.pallas_call(
         step_kernel,
         in_specs=[there] * 6,
@@ -716,7 +734,7 @@
     emb_out[...] = emb_ref[...]
 
 
-def finish(new, centres, emb_grad, rows=512):
+def finish(new, centres, emb_grad, rows=256):
     homes, width = centres.shape
     part = pl.BlockSpec((rows, width), lambda i: (i, 0))
     whole = pl.BlockSpec(emb_grad.shape, lambda i: (0, 0))

time: 157 us -> 154 us (0.981)
  Pallas kernels: 156 us -> 153 us
    pallas_call x1, Pallas kernels: 145 us -> 138 us  [step(): pl.pallas_call(step_kernel, in_specs=[there] * 6, out_specs=[there, vmem]...]
    pallas_call x1, Pallas kernels: 11.6 us -> 15.1 us  [finish(): pl.pallas_call(finish_kernel, grid=(homes // rows,), in_specs=[part, part...]
where the time goes in v5:
time: 154 us
  Pallas kernels  153 us (99%)
    pallas_call x1, Pallas kernels, step(): pl.pallas_call(step_kernel, in_specs=[there] * 6, out_specs=[there, vmem]...  138 us
    pallas_call x1, Pallas kernels, finish(): pl.pallas_call(finish_kernel, grid=(homes // rows,), in_specs=[part, part...  15.1 us

profile of v5, /device:TPU:0, one launch (start us, length us, event | category | flops | bytes accessed | tf_op | source)
XLA Modules:
  0.0 153.9 jit_solution(1900700408744080831)
XLA Ops:
  0.6 138.0 %step.1 = (f32[8,512,512]{2,1,0:T(8,128)}, f32[64,512]{1,0:T(8,128)}) custom-call(bf16[64,512]{1,0:T(8,128)(2,1)} %emb_hbm.1, s32[1,2048]{1,0:T(1,128)} %bitcast.7, s32[1,2048]{1,0:T(1,128)} %bitcast.8, s32[16,128]{1,0:T(8,128)} %bitcast.9, bf16[4096,512]{1,0:T(8,128)(2,1)} %centres_ref.1, f32[8,512,512]{2,1,0:T(8,128)} %bitcast.6), custom_call_target="tpu_custom_call" | custom-call | tf_op jit(solution)/shard_map/step/pallas_call | solution.py:698
  138.7 15.1 %finish.1 = (f32[4096,512]{1,0:T(8,128)}, bf16[4096,512]{1,0:T(8,128)(2,1)}, f32[64,512]{1,0:T(8,128)}) custom-call(f32[4096,512]{1,0:T(8,128)} %bitcast.5, bf16[4096,512]{1,0:T(8,128)(2,1)} %centres_ref.1, f32[64,512]{1,0:T(8,128)} %get-tuple-element.9.emb_ref), custom_call_target="tpu_custom_call" | custom-call | tf_op jit(solution)/shard_map/finish/pallas_call | solution.py:741

commit v6 on v5

--- a/solution.py
+++ b/solution.py
@@ -393,22 +393,29 @@
             for k, peer in enumerate(peers)
         ]
 
-    def stage_start(group, stage):
-        for copy in stage_copies(group, stage):
-            copy.start()
-
-    def stage_end(group, stage):
-        for copy in stage_copies(group, stage):
-            copy.wait()
-        slot, peers = stages[stage]
-        total = den[group, stage]
-        for k in range(len(peers)):
-            total = total + got[group, slot + k]
-        if stage < 3:
-            den[group, stage + 1] = total
-            stage_start(group, stage + 1)
-        else:
-            inverse[group] = logit_scale / total
+    def swap_inverse(group):
+        ref = inverse.at[group]
+        return remote(ref, ref, den_sent.at[20 + group], den_came.at[20 + group], partner)
+
+    def sum_denominators():
+        stage_copies(other, 0)[0].start()
+        stage_copies(c, 0)[0].wait_recv()
+        den[c, 1] = den[c, 0] + got[c, 0]
+        for stage in range(1, 4):
+            copies = stage_copies(c, stage)
+            for copy in copies:
+                copy.start()
+            for copy in copies:
+                copy.wait_recv()
+            total = den[c, stage]
+            for k in range(len(copies)):
+                total = total + got[c, stages[stage][0] + k]
+            if stage < 3:
+                den[c, stage + 1] = total
+            else:
+                inverse[c] = logit_scale / total
+        swap_inverse(c).start()
+        swap_inverse(other).wait_recv()
 
     def gradients(group, i):
         for side in range(2):
@@ -448,24 +455,17 @@
     def _(i):
         exponents(0, i)
 
-    stage_start(0, 0)
-
     @pl.loop(4, pieces)
     def _(i):
         exponents(1, i)
 
-    stage_start(1, 0)
-    for n in range(3):
-        stage_end(0, n)
-        stage_end(1, n)
-    stage_end(0, 3)
+    sum_denominators()
 
     @pl.loop(0, 4)
     def _(i):
         gradients(0, i)
         give_over(i)
 
-    stage_end(1, 3)
     @pl.loop(4, pieces)
     def _(i):
         gradients(1, i)
@@ -664,6 +664,11 @@
         onward(n).wait_send()
     for part in (0, 1):
         swap_part(part, c).wait_send()
+    stage_copies(other, 0)[0].wait_send()
+    for stage in range(1, 4):
+        for copy in stage_copies(c, stage):
+            copy.wait_send()
+    swap_inverse(c).wait_send()
 
     @pl.loop(0, pieces)
     def _(i):
@@ -694,7 +699,7 @@
     sums = [(2, 4, blocks // 2, block), (2, 10, blocks // 2, block), (2, blocks // 2, block), (kept, width)]
     halves = [(blocks, width, lanes)] * 2 + [(ACROSS, ACROSS, width, lanes)] + [(3, 2, 2, half, lanes)] * 2
     halves += [(ACROSS, half, lanes)] * 2 + [(3, 2, half // 2, lanes)] * 2 + [(ACROSS, rows, width), (3, rows, width)]
-    sems = [24, N_TILES, N_TILES, N_TILES, N_TILES, 6, 6, 54, 54, 10, 10, 20, 20, N_TILES, N_TILES, 12, 12, 8, 8, 27, 27]
+    sems = [24, N_TILES, N_TILES, N_TILES, N_TILES, 6, 6, 54, 54, 11, 11, 22, 22, N_TILES, N_TILES, 12, 12, 8, 8, 27, 27]
     return pl.pallas_call(
         step_kernel,
         in_specs=[there] * 6,
@@ -734,7 +739,7 @@
     emb_out[...] = emb_ref[...]
 
 
-def finish(new, centres, emb_grad, rows=256):
+def finish(new, centres, emb_grad, rows=1024):
     homes, width = centres.shape
     part = pl.BlockSpec((rows, width), lambda i: (i, 0))
     whole = pl.BlockSpec(emb_grad.shape, lambda i: (0, 0))

time: 154 us -> 153 us (level)
    pallas_call x1, Pallas kernels: 15.1 us -> 9.89 us  [finish(): pl.pallas_call(finish_kernel, grid=(homes // rows,), in_specs=[part, part...]
    pallas_call x1, Pallas kernels: 138 us -> 143 us  [step(): pl.pallas_call(step_kernel, in_specs=[there] * 6, out_specs=[there, vmem]...]
where the time goes in v6:
time: 153 us
  Pallas kernels  152 us (99%)
    pallas_call x1, Pallas kernels, step(): pl.pallas_call(step_kernel, in_specs=[there] * 6, out_specs=[there, vmem]...  143 us
    pallas_call x1, Pallas kernels, finish(): pl.pallas_call(finish_kernel, grid=(homes // rows,), in_specs=[part, part...  9.89 us

profile of v6, /device:TPU:0, one launch (start us, length us, event | category | flops | bytes accessed | tf_op | source)
XLA Modules:
  0.0 153.1 jit_solution(16622173170117334038)
XLA Ops:
  0.6 142.5 %step.1 = (f32[8,512,512]{2,1,0:T(8,128)}, f32[64,512]{1,0:T(8,128)}) custom-call(bf16[64,512]{1,0:T(8,128)(2,1)} %emb_hbm.1, s32[1,2048]{1,0:T(1,128)} %bitcast.7, s32[1,2048]{1,0:T(1,128)} %bitcast.8, s32[16,128]{1,0:T(8,128)} %bitcast.9, bf16[4096,512]{1,0:T(8,128)(2,1)} %centres_ref.1, f32[8,512,512]{2,1,0:T(8,128)} %bitcast.6), custom_call_target="tpu_custom_call" | custom-call | tf_op jit(solution)/shard_map/step/pallas_call | solution.py:703
  143.2 9.9 %finish.1 = (f32[4096,512]{1,0:T(8,128)}, bf16[4096,512]{1,0:T(8,128)(2,1)}, f32[64,512]{1,0:T(8,128)}) custom-call(f32[4096,512]{1,0:T(8,128)} %bitcast.5, bf16[4096,512]{1,0:T(8,128)(2,1)} %centres_ref.1, f32[64,512]{1,0:T(8,128)} %get-tuple-element.9.emb_ref), custom_call_target="tpu_custom_call" | custom-call | tf_op jit(solution)/shard_map/finish/pallas_call | solution.py:746
